TPU v7x, 256 devices: a whole 4x4x8 slice. The times are simulated.
256 devices in a mesh: domain: 32 (over z, y_hi, core), band: 8 (over x, y_lo).
Axes of the slice: x: 4, y: 4 (y_hi: 2, y_lo: 2; y = y_hi * 2 + y_lo), z: 8, core: 2. Of those that a mesh axis runs over, the one named last changes fastest.
Arguments:
- orbitals: float32 [32, 192, 36864], P('band', 'domain'), may hold values from -6 to 6
- potential: float32 [192, 36864], P('domain'), may hold values from -1.5 to 1.5
- coefficients: float32 [32, 32], replicated, may hold values from -1.75 to 1.75
- owners: int32 [2], replicated, may hold values from 0 to 31
Outputs:
- filtered: float32 [32, 192, 36864], P('band', 'domain')
- rotated: float32 [32, 192, 36864], P('band', 'domain')
All inputs are finite; a program needn't handle non-finite values.
Results may differ from a plain program's by a relative error of at most 0.0001.
Values sent between devices are 32-bit elements; how exact they have to be, the bound alone decides.
No kernel may reach another device: no remote copies, remote signals or barrier semaphores. Data moves between devices by JAX's collectives and lax.ppermute only.
A program may use at most 256 MiB of HBM per device.

v0:
```python
import jax
import jax.numpy as jnp
from jax import lax
from jax.sharding import PartitionSpec as P

NZ = 192
DEG = 3


lap_coeffs = (-205.0 / 72.0, 8.0 / 5.0, -1.0 / 5.0, 8.0 / 315.0, -1.0 / 560.0)


def extended_2(x, sides, width):
    for axis, dim in sides:
        peers, length = (lax.axis_size(axis), x.shape[dim])
        up = [(i, (i + 1) % peers) for i in range(peers)]
        down = [(j, i) for i, j in up]
        last = lax.slice_in_dim(x, length - width, length, axis=dim)
        first = lax.slice_in_dim(x, 0, width, axis=dim)
        before = lax.ppermute(last, axis, up)
        after = lax.ppermute(first, axis, down)
        x = jnp.concatenate([before, x, after], axis=dim)
    return x


def spread(value, axis, source):
    kept = jnp.where(lax.axis_index(axis) == source, value, 0).astype(value.dtype)
    return lax.psum(kept, axis)


def hamiltonian(field, extended, potential):
    cells_x = field.shape[1]
    plane = field.shape[2]
    column_z = jnp.arange(plane) % NZ
    padded_y = jnp.pad(field, ((0, 0), (0, 0), (4 * NZ, 4 * NZ)))
    padded_z = jnp.pad(field, ((0, 0), (0, 0), (4, 4)))
    summed = 3.0 * lap_coeffs[0] * field
    for shift in range(1, 5):
        weight_k = lap_coeffs[shift]
        upper_ok = (column_z + shift < NZ).astype(field.dtype)
        lower_ok = (column_z - shift >= 0).astype(field.dtype)
        summed = summed + weight_k * (
            extended[:, 4 + shift : 4 + shift + cells_x]
            + extended[:, 4 - shift : 4 - shift + cells_x]
        )
        summed = summed + weight_k * (
            padded_y[:, :, (4 + shift) * NZ : (4 + shift) * NZ + plane]
            + padded_y[:, :, (4 - shift) * NZ : (4 - shift) * NZ + plane]
        )
        summed = summed + weight_k * (
            padded_z[:, :, 4 + shift : 4 + shift + plane] * upper_ok
            + padded_z[:, :, 4 - shift : 4 - shift + plane] * lower_ok
        )
    return -0.5 * summed + potential[None] * field


def chebyshev(block, potential, widen):
    previous = block
    current = (hamiltonian(block, widen(block), potential) - 6.0 * block) / 5.0
    for level in range(DEG - 1):
        following = (
            2.0 * (hamiltonian(current, widen(current), potential) - 6.0 * current) / 5.0 - previous
        )
        previous = current
        current = following
    return current


def widen_own(field):
    return extended_2(field, (("domain", 1),), 4)


def mixing(block, coefficients, source, target, width):
    part_coeffs = lax.dynamic_slice(coefficients, (source * width, target * width), (width, width))
    return jnp.einsum("bxp,bc->cxp", block, part_coeffs, precision=lax.Precision.HIGHEST)


def body(orbitals, potential, coefficients, owners):
    width = orbitals.shape[0]
    rounds_count = owners.shape[0]
    mine = lax.axis_index("band")
    sources = owners // width
    offsets = owners % width
    filtered = chebyshev(orbitals, potential, widen_own)
    rotated = mixing(filtered, coefficients, mine, mine, width)
    for turn in range(rounds_count):
        arrived = spread(filtered, "band", sources[turn])
        rolled = jnp.roll(arrived, -offsets[turn], axis=0)
        rotated = rotated + mixing(rolled, coefficients, sources[turn], mine, width)
    return (filtered, rotated)


def solution(mesh):
    in_specs = (P("band", "domain", None), P("domain", None), P(), P())
    out_specs = (P("band", "domain", None), P("band", "domain", None))
    return jax.shard_map(body, mesh=mesh, in_specs=in_specs, out_specs=out_specs, check_vma=False)
```

profile of v0, /device:TPU:16, one launch (start us, length us, event | category | flops | bytes accessed | tf_op | source)
XLA Modules:
  0.0 609.4 jit_solution(5512087887906080027)
XLA Ops:
  7.2 2.7 fusion.148
  10.1 3.2 collective-permute-start
  13.4 0.8 fusion.127
  14.2 0.8 fusion.129
  15.0 0.8 fusion.131
  15.8 49.3 %collective-permute-done.1 = f32[4,4,36864]{2,0,1:T(4,128)S(1)} collective-permute-done((f32[4,4,36864]{2,0,1:T(4,128)S(1)}, f32[4,4,36864]{2,0,1:T(4,128)S(1)}, u32[]{:S(2)}, u32[]{:S(2)}) %collective-permute-start.1) | collective-permute-done | bytes 2359328 | tf_op jit(solution)/shard_map/ppermute | solution.py:20
  65.3 1.1 constant_dynamic-update-slice_fusion.1
  66.4 0.3 constant_dynamic-update-slice_fusion
  66.7 28.5 %broadcast_multiply_fusion = (f32[4,6,36864]{2,0,1:T(4,128)S(1)}, f32[4,6,36864]{2,0,1:T(4,128)}) fusion(f32[4,6,36864]{2,0,1:T(4,128)S(1)} %copy-done.1, f32[6,36864]{1,0:T(8,128)} %param.7, f32[36864]{0:T(1024)} %get-tuple-element.32, f32[36864]{0:T(1024)} %get-tuple-element.31, f32[4,10,36864]{2,0,1:T(4,128)S(1)} %get-tuple-element.16, ...), kind=kLoop, calls=%fused_computation.196 | loop fusion | flops 45121536 | bytes 40992768 | tf_op jit(solution)/shard_map/div | solution.py:59
  95.3 0.6 fusion.147
  95.9 2.0 collective-permute-start.2
  98.0 51.5 %collective-permute-done.2 = f32[4,4,36864]{2,0,1:T(4,128)S(1)} collective-permute-done((f32[4,4,36864]{2,0,1:T(4,128)S(1)}, f32[4,4,36864]{2,0,1:T(4,128)S(1)}, u32[]{:S(2)}, u32[]{:S(2)}) %collective-permute-start.2) | collective-permute-done | bytes 2359328 | tf_op jit(solution)/shard_map/ppermute | solution.py:21
  149.6 26.8 %multiply_subtract_fusion.1 = f32[4,6,36864]{2,0,1:T(4,128)S(1)} fusion(f32[4,6,36864]{2,0,1:T(4,128)S(1)} %copy-done.1, f32[4,6,36864]{2,0,1:T(4,128)S(1)} %copy-done.4, f32[4,6,36864]{2,0,1:T(4,128)S(1)} %get-tuple-element.7, f32[4,4,36864]{2,0,1:T(4,128)S(1)} %collective-permute-done.3, f32[4,4,36864]{2,0,1:T(4,128)S(1)} %collective-permute-done.2, ...), kind=kLoop, calls=%fused_computation.142 | loop fusion | flops 53084160 | bytes 20938752 | tf_op jit(solution)/shard_map/sub | solution.py:62
  176.4 3.2 fusion.146
  179.7 3.4 collective-permute-start.4
  183.1 0.7 fusion.149
  185.0 49.8 %collective-permute-done.4 = f32[4,4,36864]{2,0,1:T(4,128)S(1)} collective-permute-done((f32[4,4,36864]{2,0,1:T(4,128)}, f32[4,4,36864]{2,0,1:T(4,128)S(1)}, u32[]{:S(2)}, u32[]{:S(2)}) %collective-permute-start.4) | collective-permute-done | bytes 2359328 | tf_op jit(solution)/shard_map/ppermute | solution.py:21
  234.9 1.4 copy-done.15
  236.3 46.0 %broadcast_select_fusion = (f32[4,6,36864]{2,0,1:T(4,128)}, f32[4,6,36864]{2,0,1:T(4,128)S(1)}) fusion(pred[]{:T(512)S(6)} %eq.15, f32[4,6,36864]{2,0,1:T(4,128)} %get-tuple-element.8, f32[4,6,36864]{2,0,1:T(4,128)} %copy-done.2, f32[6,36864]{1,0:T(8,128)} %param.7, f32[36864]{0:T(1024)} %get-tuple-element.32, f32[36864]{0:T(1024)} %get-tuple-element.31, ...), kind=kLoop, calls=%fused_computation.194 | loop fusion | flops 54853632 | bytes 20938752 | tf_op jit(solution)/shard_map/jit(_where)/select_n | solution.py:27
  282.3 3.0 broadcast_select_fusion.1
  288.0 8.9 %fusion.136 = f32[4,6,36864]{2,0,1:T(4,128)} fusion(f32[4,6,36864]{2,0,1:T(4,128)S(1)} %get-tuple-element.6, f32[32,32]{1,0:T(8,128)S(1)} %copy-done, s32[]{:T(128)S(6)} %select_n.129), kind=kOutput, calls=%fused_computation.225 | convolution fusion | flops 42467328 | bytes 7079940 | tf_op jit(solution)/shard_map/bxp,bc->cxp/dot_general | solution.py:75
  296.9 281.5 %all-reduce.9.cloned.1.call-done = (f32[4,6,36864]{2,0,1:T(4,128)}, f32[4,6,36864]{2,0,1:T(4,128)}) async-done(((f32[4,6,36864]{2,0,1:T(4,128)}, f32[4,6,36864]{2,0,1:T(4,128)}), (f32[4,6,36864]{2,0,1:T(4,128)}, f32[4,6,36864]{2,0,1:T(4,128)})) %all-reduce.9.cloned.1.call-update) | async-done | bytes 7077904 | tf_op jit(solution)/shard_map/psum | solution.py:28
  578.4 12.4 %convolution_add_fusion.1 = f32[4,6,36864]{2,0,1:T(4,128)S(1)} fusion(f32[4,6,36864]{2,0,1:T(4,128)} %fusion.136, s32[]{:T(128)S(6)} %select_n.141, f32[4,6,36864]{2,0,1:T(4,128)} %get-tuple-element.3, f32[32,32]{1,0:T(8,128)S(1)} %copy-done, s32[]{:T(128)S(6)} %select_n.131, s32[]{:T(128)S(6)} %select_n.129), kind=kOutput, calls=%fused_computation.1 | convolution fusion | flops 44236800 | bytes 10618892 | tf_op jit(solution)/shard_map/bxp,bc->cxp/dot_general | solution.py:75
  590.8 11.7 %convolution_add_fusion = f32[4,6,36864]{2,0,1:T(4,128)} fusion(f32[4,6,36864]{2,0,1:T(4,128)S(1)} %convolution_add_fusion.1, s32[]{:T(128)S(6)} %select_n.143, f32[4,6,36864]{2,0,1:T(4,128)S(1)} %copy-done.6, f32[32,32]{1,0:T(8,128)S(1)} %copy-done, s32[]{:T(128)S(6)} %select_n.135, s32[]{:T(128)S(6)} %select_n.129), kind=kOutput, calls=%fused_computation | convolution fusion | flops 44236800 | bytes 10618892 | tf_op jit(solution)/shard_map/bxp,bc->cxp/dot_general | solution.py:75
  (45 shorter events, 0.7 us)
Async XLA Ops:
  7.2 280.8 %copy-start = (f32[32,32]{1,0:T(8,128)S(1)}, f32[32,32]{1,0:T(8,128)}, u32[]{:S(2)}) copy-start(f32[32,32]{1,0:T(8,128)} %param.8) | copy-start | bytes 12292
  7.2 571.2 %all-reduce.9.cloned.1.call-start = ((), (), s32[]{:S(2)}) async-start(), calls=%async_computation | async-start | bytes 14155776 | tf_op jit(solution)/shard_map/psum | solution.py:28
  10.0 55.3 %copy-start.1 = (f32[4,6,36864]{2,0,1:T(4,128)S(1)}, f32[4,6,36864]{2,0,1:T(4,128)}, u32[]{:S(2)}) copy-start(f32[4,6,36864]{2,0,1:T(4,128)} %param.6) | copy-start | bytes 10616836
  10.0 55.1 %collective-permute-start.1 = (f32[4,4,36864]{2,0,1:T(4,128)S(1)}, f32[4,4,36864]{2,0,1:T(4,128)S(1)}, u32[]{:S(2)}, u32[]{:S(2)}) collective-permute-start(f32[4,4,36864]{2,0,1:T(4,128)S(1)} %get-tuple-element.14), channel_id=1, source_target_pairs={{0,8},{8,16},{16,24},{24,32},{32,40},{40,48},{48,56},{56,64},{64,7... | collective-permute-start | bytes 7077896 | tf_op jit(solution)/shard_map/ppermute | solution.py:20
  10.1 56.4 %collective-permute-start = (f32[4,4,36864]{2,0,1:T(4,128)S(1)}, f32[4,4,36864]{2,0,1:T(4,128)S(1)}, u32[]{:S(2)}, u32[]{:S(2)}) collective-permute-start(f32[4,4,36864]{2,0,1:T(4,128)S(1)} %get-tuple-element.13), channel_id=1, source_target_pairs={{8,0},{16,8},{24,16},{32,24},{40,32},{48,40},{56,48},{64,56},{72,6... | collective-permute-start | bytes 7077896 | tf_op jit(solution)/shard_map/ppermute | solution.py:21
  13.4 136.1 %copy-start.7 = (f32[36864]{0:T(1024)}, f32[36864]{0:T(1024)S(1)}, u32[]{:S(2)}) copy-start(f32[36864]{0:T(1024)S(1)} %get-tuple-element.25) | copy-start | bytes 442372
  13.4 136.1 %copy-start.8 = (f32[36864]{0:T(1024)}, f32[36864]{0:T(1024)S(1)}, u32[]{:S(2)}) copy-start(f32[36864]{0:T(1024)S(1)} %get-tuple-element.26) | copy-start | bytes 442372
  14.2 135.4 %copy-start.9 = (f32[36864]{0:T(1024)}, f32[36864]{0:T(1024)S(1)}, u32[]{:S(2)}) copy-start(f32[36864]{0:T(1024)S(1)} %get-tuple-element.27) | copy-start | bytes 442372
  95.2 2.7 copy-start.5
  95.2 54.3 %copy-start.4 = (f32[4,6,36864]{2,0,1:T(4,128)S(1)}, f32[4,6,36864]{2,0,1:T(4,128)}, u32[]{:S(2)}) copy-start(f32[4,6,36864]{2,0,1:T(4,128)} %get-tuple-element.8) | copy-start | bytes 10616836
  95.2 54.3 %copy-start.10 = (f32[36864]{0:T(1024)S(1)}, f32[36864]{0:T(1024)}, u32[]{:S(2)}) copy-start(f32[36864]{0:T(1024)} %get-tuple-element.28) | copy-start | bytes 442372
  95.2 54.3 %copy-start.11 = (f32[36864]{0:T(1024)S(1)}, f32[36864]{0:T(1024)}, u32[]{:S(2)}) copy-start(f32[36864]{0:T(1024)} %get-tuple-element.29) | copy-start | bytes 442372
  95.3 54.3 %copy-start.12 = (f32[36864]{0:T(1024)S(1)}, f32[36864]{0:T(1024)}, u32[]{:S(2)}) copy-start(f32[36864]{0:T(1024)} %get-tuple-element.30) | copy-start | bytes 442372
  95.3 54.3 %copy-start.13 = (f32[36864]{0:T(1024)S(1)}, f32[36864]{0:T(1024)}, u32[]{:S(2)}) copy-start(f32[36864]{0:T(1024)} %get-tuple-element.31) | copy-start | bytes 442372
  95.3 54.3 %copy-start.14 = (f32[36864]{0:T(1024)S(1)}, f32[36864]{0:T(1024)}, u32[]{:S(2)}) copy-start(f32[36864]{0:T(1024)} %get-tuple-element.32) | copy-start | bytes 442372
  95.9 53.6 %collective-permute-start.2 = (f32[4,4,36864]{2,0,1:T(4,128)S(1)}, f32[4,4,36864]{2,0,1:T(4,128)S(1)}, u32[]{:S(2)}, u32[]{:S(2)}) collective-permute-start(f32[4,4,36864]{2,0,1:T(4,128)S(1)} %get-tuple-element.11), channel_id=1, source_target_pairs={{8,0},{16,8},{24,16},{32,24},{40,32},{48,40},{56,48},{64,56},{72,6... | collective-permute-start | bytes 7077896 | tf_op jit(solution)/shard_map/ppermute | solution.py:21
  97.9 51.6 %collective-permute-start.3 = (f32[4,4,36864]{2,0,1:T(4,128)S(1)}, f32[4,4,36864]{2,0,1:T(4,128)S(1)}, u32[]{:S(2)}, u32[]{:S(2)}) collective-permute-start(f32[4,4,36864]{2,0,1:T(4,128)S(1)} %get-tuple-element.12), channel_id=1, source_target_pairs={{0,8},{8,16},{16,24},{24,32},{32,40},{40,48},{48,56},{56,64},{64,7... | collective-permute-start | bytes 7077896 | tf_op jit(solution)/shard_map/ppermute | solution.py:20
  176.4 3.3 copy-start.2
  176.4 6.7 %copy-start.16 = (s32[2]{0:T(128)S(1)}, s32[2]{0:T(128)}, u32[]{:S(2)}) copy-start(s32[2]{0:T(128)} %param.9) | copy-start | bytes 28
  179.7 55.2 %collective-permute-start.4 = (f32[4,4,36864]{2,0,1:T(4,128)}, f32[4,4,36864]{2,0,1:T(4,128)S(1)}, u32[]{:S(2)}, u32[]{:S(2)}) collective-permute-start(f32[4,4,36864]{2,0,1:T(4,128)} %get-tuple-element.9), channel_id=1, source_target_pairs={{8,0},{16,8},{24,16},{32,24},{40,32},{48,40},{56,48},{64,56},{72,6... | collective-permute-start | bytes 7077896 | tf_op jit(solution)/shard_map/ppermute | solution.py:21
  183.1 53.2 %collective-permute-start.5 = (f32[4,4,36864]{2,0,1:T(4,128)}, f32[4,4,36864]{2,0,1:T(4,128)}, u32[]{:S(2)}, u32[]{:S(2)}) collective-permute-start(f32[4,4,36864]{2,0,1:T(4,128)} %get-tuple-element.10), channel_id=1, source_target_pairs={{0,8},{8,16},{16,24},{24,32},{32,40},{40,48},{48,56},{56,64},{64,7... | collective-permute-start | bytes 7077896 | tf_op jit(solution)/shard_map/ppermute | solution.py:20
  234.9 1.4 copy-start.15
  282.3 5.7 copy-start.3
  578.4 12.4 %copy-start.6 = (f32[4,6,36864]{2,0,1:T(4,128)S(1)}, f32[4,6,36864]{2,0,1:T(4,128)}, u32[]{:S(2)}) copy-start(f32[4,6,36864]{2,0,1:T(4,128)} %get-tuple-element.4) | copy-start | bytes 10616836
Sparse Core Ops, SparseCore 0:
  285.5 292.8 all-reduce.8
where the time goes:
time: 614 us; the launch traced here: 609 us
  waiting for transfers between devices  432 us (70%)
  other arithmetic  107 us (17%)
  matrix products  33 us (5%)
  between operations  18.2 us (3%)
  local copies, waits for them, and re-layouts  10.3 us (2%)
  starting transfers between devices  8.78 us (1%)
    psum x1, waiting for transfers between devices, spread(): return lax.psum(kept, axis)  281 us
    ppermute x3, waiting for transfers between devices, extended_2(): after = lax.ppermute(first, axis, down)  101 us
    ppermute x3, waiting for transfers between devices, extended_2(): before = lax.ppermute(last, axis, up)  49.3 us
    select_n x2, other arithmetic, spread(): jnp.where(lax.axis_index(axis) == source, value, 0).astype(value.dtype)  49 us
    dot_general x3, matrix products, mixing(): jnp.einsum('bxp,bc->cxp', block, part_coeffs, precision=lax.Precision.HIG...  33 us
    div x1, other arithmetic, chebyshev(): current = (hamiltonian(block, widen(block), potential) - 6.0 * block) / 5.0  28.5 us
    sub x1, other arithmetic, chebyshev(): 2.0 * (hamiltonian(current, widen(current), potential) - 6.0 * current)  26.8 us
  transfers between devices with their start and end apart: 7, of which 4 were waited for; matrix products, arithmetic and copies ran while one was open for 2% of the time, Pallas kernels for 0%

commit v1 on v0

--- a/solution.py
+++ b/solution.py
@@ -21,11 +21,6 @@
         after = lax.ppermute(first, axis, down)
         x = jnp.concatenate([before, x, after], axis=dim)
     return x
-
-
-def spread(value, axis, source):
-    kept = jnp.where(lax.axis_index(axis) == source, value, 0).astype(value.dtype)
-    return lax.psum(kept, axis)
 
 
 def hamiltonian(field, extended, potential):
@@ -70,24 +65,31 @@
     return extended_2(field, (("domain", 1),), 4)
 
 
-def mixing(block, coefficients, source, target, width):
-    part_coeffs = lax.dynamic_slice(coefficients, (source * width, target * width), (width, width))
-    return jnp.einsum("bxp,bc->cxp", block, part_coeffs, precision=lax.Precision.HIGHEST)
+def mixing_matrix(coefficients, owners, width):
+    rows = jnp.arange(coefficients.shape[0])
+    same = (rows[:, None] // width) == (rows[None, :] // width)
+    mixed = jnp.where(same, coefficients, 0.0)
+    for turn in range(owners.shape[0]):
+        source = owners[turn] // width
+        offset = owners[turn] % width
+        member = (rows // width == source)[:, None]
+        from_row = source * width + (rows % width - offset) % width
+        picks = (from_row[:, None] == rows[None, :]).astype(coefficients.dtype)
+        part = jnp.dot(picks, coefficients, precision=lax.Precision.HIGHEST)
+        mixed = mixed + jnp.where(member, part, 0.0)
+    return mixed
 
 
 def body(orbitals, potential, coefficients, owners):
-    width = orbitals.shape[0]
-    rounds_count = owners.shape[0]
-    mine = lax.axis_index("band")
-    sources = owners // width
-    offsets = owners % width
+    width, planes, cells = orbitals.shape
+    bands = lax.axis_size("band")
     filtered = chebyshev(orbitals, potential, widen_own)
-    rotated = mixing(filtered, coefficients, mine, mine, width)
-    for turn in range(rounds_count):
-        arrived = spread(filtered, "band", sources[turn])
-        rolled = jnp.roll(arrived, -offsets[turn], axis=0)
-        rotated = rotated + mixing(rolled, coefficients, sources[turn], mine, width)
-    return (filtered, rotated)
+    mixed = mixing_matrix(coefficients, owners, width).reshape(bands, width, bands, width)
+    parts = filtered.reshape(width, planes, bands, cells // bands)
+    gathered = lax.all_to_all(parts, "band", 2, 0)
+    turned = jnp.einsum("iqxp,iqjo->joxp", gathered, mixed, precision=lax.Precision.HIGHEST)
+    rotated = lax.all_to_all(turned, "band", 0, 2)
+    return (filtered, rotated.reshape(width, planes, cells))
 
 
 def solution(mesh):

time: 614 us -> 352 us (0.57)
  waiting for transfers between devices: 432 us -> 182 us
  blocking collectives: 0 us -> 27.1 us
  matrix products: 33 us -> 10.6 us
  other arithmetic: 107 us -> 86.2 us
  local copies, waits for them, and re-layouts: 10.3 us -> 25 us
  between operations: 18.2 us -> 6.37 us
    psum x1 -> x0, waiting for transfers between devices: 281 us -> none  [spread(): return lax.psum(kept, axis)]
    select_n x3 -> x1, other arithmetic: 49 us -> 0.02 us  [mixing_matrix(): same = rows[:, None] // width == rows[None, :] // width]
    all_to_all x0 -> x1, waiting for transfers between devices: none -> 29.6 us  [body(): gathered = lax.all_to_all(parts, 'band', 2, 0)]
    sub x1 -> x2, other arithmetic: 26.8 us -> 55.6 us  [chebyshev(): 2.0 * (hamiltonian(current, widen(current), potential) - 6.0 * current)]
    all_to_all x0 -> x1, blocking collectives: none -> 27.1 us  [body(): rotated = lax.all_to_all(turned, 'band', 0, 2)]
    dot_general x3, matrix products: 33 us -> 10.6 us  [the longest x1 8.7 us: body(): jnp.einsum('iqxp,iqjo->joxp', gathered, mixed, precision=lax.Precision.HI...]
    another operation x0 -> x3, local copies, waits for them, and re-layouts: none -> 11.9 us  [the longest x2 8.25 us: body(): gathered = lax.all_to_all(parts, 'band', 2, 0)]
  transfers between devices with their start and end apart: 7 -> 7, of which waited for: 4 -> 4; matrix products, arithmetic and copies ran while one was open for 2% -> 3% of each run, Pallas kernels for 0% -> 0%
where the time goes in v1:
time: 352 us; the launch traced here: 351 us
  waiting for transfers between devices  182 us (52%)
  other arithmetic  86.2 us (24%)
  blocking collectives  27.1 us (8%)
  local copies, waits for them, and re-layouts  25 us (7%)
  starting transfers between devices  14.2 us (4%)
  matrix products  10.6 us (3%)
  between operations  6.37 us (2%)
    ppermute x3, waiting for transfers between devices, extended_2(): after = lax.ppermute(first, axis, down)  103 us
    sub x2, other arithmetic, chebyshev(): 2.0 * (hamiltonian(current, widen(current), potential) - 6.0 * current)  55.6 us
    ppermute x3, waiting for transfers between devices, extended_2(): before = lax.ppermute(last, axis, up)  49.4 us
    all_to_all x1, waiting for transfers between devices, body(): gathered = lax.all_to_all(parts, 'band', 2, 0)  29.6 us
    div x1, other arithmetic, chebyshev(): current = (hamiltonian(block, widen(block), potential) - 6.0 * block) / 5.0  27.9 us
    all_to_all x1, blocking collectives, body(): rotated = lax.all_to_all(turned, 'band', 0, 2)  27.1 us
    ppermute x3, starting transfers between devices, extended_2(): after = lax.ppermute(first, axis, down)  8.73 us
    dot_general x1, matrix products, body(): jnp.einsum('iqxp,iqjo->joxp', gathered, mixed, precision=lax.Precision.HI...  8.7 us
  transfers between devices with their start and end apart: 7, of which 4 were waited for; matrix products, arithmetic and copies ran while one was open for 3% of the time, Pallas kernels for 0%

profile of v1, /device:TPU:16, one launch (start us, length us, event | category | flops | bytes accessed | tf_op | source)
XLA Modules:
  0.0 351.3 jit_solution(15616232960353589516)
XLA Ops:
  0.6 2.7 fusion.143
  3.5 3.2 collective-permute-start
  7.6 0.8 fusion.129
  9.2 49.3 %collective-permute-done.1 = f32[4,4,36864]{2,0,1:T(4,128)S(1)} collective-permute-done((f32[4,4,36864]{2,0,1:T(4,128)S(1)}, f32[4,4,36864]{2,0,1:T(4,128)S(1)}, u32[]{:S(2)}, u32[]{:S(2)}) %collective-permute-start.1) | collective-permute-done | bytes 2359328 | tf_op jit(solution)/shard_map/ppermute | solution.py:20
  58.7 1.1 constant_dynamic-update-slice_fusion.1
  60.2 27.9 %broadcast_multiply_fusion = (f32[4,6,36864]{2,0,1:T(4,128)S(1)}, f32[4,6,36864]{2,0,1:T(4,128)}) fusion(f32[4,6,36864]{2,0,1:T(4,128)S(1)} %copy-done, f32[6,36864]{1,0:T(8,128)} %param.5, f32[36864]{0:T(1024)} %get-tuple-element.23, f32[36864]{0:T(1024)} %get-tuple-element.22, f32[4,10,36864]{2,0,1:T(4,128)S(1)} %get-tuple-element.13, ...), kind=kLoop, calls=%fused_computation.189 | loop fusion | flops 45121536 | bytes 40992768 | tf_op jit(solution)/shard_map/div | solution.py:54
  88.7 2.0 collective-permute-start.2
  90.9 51.5 %collective-permute-done.2 = f32[4,4,36864]{2,0,1:T(4,128)S(1)} collective-permute-done((f32[4,4,36864]{2,0,1:T(4,128)S(1)}, f32[4,4,36864]{2,0,1:T(4,128)S(1)}, u32[]{:S(2)}, u32[]{:S(2)}) %collective-permute-start.2) | collective-permute-done | bytes 2359328 | tf_op jit(solution)/shard_map/ppermute | solution.py:21
  142.4 26.6 %multiply_subtract_fusion.1 = f32[4,6,36864]{2,0,1:T(4,128)S(1)} fusion(f32[4,6,36864]{2,0,1:T(4,128)S(1)} %copy-done, f32[4,6,36864]{2,0,1:T(4,128)S(1)} %copy-done.1, f32[4,6,36864]{2,0,1:T(4,128)S(1)} %get-tuple-element.4, f32[4,4,36864]{2,0,1:T(4,128)S(1)} %collective-permute-done.3, f32[4,4,36864]{2,0,1:T(4,128)S(1)} %collective-permute-done.2, ...), kind=kLoop, calls=%fused_computation.137 | loop fusion | flops 53084160 | bytes 20938752 | tf_op jit(solution)/shard_map/sub | solution.py:57
  169.6 3.5 collective-permute-start.4
  173.1 51.4 %collective-permute-done.4 = f32[4,4,36864]{2,0,1:T(4,128)S(1)} collective-permute-done((f32[4,4,36864]{2,0,1:T(4,128)S(1)}, f32[4,4,36864]{2,0,1:T(4,128)S(1)}, u32[]{:S(2)}, u32[]{:S(2)}) %collective-permute-start.4) | collective-permute-done | bytes 2359328 | tf_op jit(solution)/shard_map/ppermute | solution.py:21
  224.5 29.1 %multiply_subtract_fusion = f32[4,6,36864]{2,0,1:T(4,128)} fusion(f32[4,6,36864]{2,0,1:T(4,128)S(1)} %multiply_subtract_fusion.1, f32[4,4,36864]{2,0,1:T(4,128)S(1)} %collective-permute-done.5, f32[4,4,36864]{2,0,1:T(4,128)S(1)} %collective-permute-done.4, f32[6,36864]{1,0:T(8,128)S(1)} %copy-done.2, f32[36864]{0:T(1024)S(1)} %copy-done.7, ...), kind=kLoop, calls=%fused_computation.106 | loop fusion | flops 53968896 | bytes 17399808 | tf_op jit(solution)/shard_map/sub | solution.py:57
  253.6 4.2 %broadcast_in_dim_reshape.3 = f32[1,4,6,8,4608]{4,3,1,2,0:T(8,128)S(1)} reshape(f32[4,6,36864]{2,0,1:T(4,128)} %multiply_subtract_fusion) | data formatting | bytes 7077888 | tf_op jit(solution)/shard_map/broadcast_in_dim;reshape | solution.py:89
  257.8 4.1 %copy.19 = f32[1,4,6,8,4608]{4,1,2,0,3:T(4,128)} copy(f32[1,4,6,8,4608]{4,3,1,2,0:T(8,128)S(1)} %broadcast_in_dim_reshape.3) | data formatting | bytes 7077888 | tf_op jit(solution)/shard_map/broadcast_in_dim;reshape | solution.py:89
  261.9 5.4 %all-to-all-start = ((f32[1,4,6,8,4608]{4,1,2,0,3:T(4,128)}), f32[1,4,6,8,4608]{4,1,2,0,3:T(4,128)S(1)}, u32[]{:S(2)}, u32[]{:S(2)}) async-start(f32[1,4,6,8,4608]{4,1,2,0,3:T(4,128)} %copy.19), calls=%async_computation | async-start | bytes 7077888 | tf_op jit(solution)/shard_map/all_to_all | solution.py:89
  273.4 1.0 fusion.122
  274.4 0.9 fusion.121
  276.1 1.8 copy.24
  277.9 29.6 %all-to-all-done = f32[1,4,6,8,4608]{4,1,2,0,3:T(4,128)S(1)} async-done(((f32[1,4,6,8,4608]{4,1,2,0,3:T(4,128)}), f32[1,4,6,8,4608]{4,1,2,0,3:T(4,128)S(1)}, u32[]{:S(2)}, u32[]{:S(2)}) %all-to-all-start) | async-done | bytes 3538976 | tf_op jit(solution)/shard_map/all_to_all | solution.py:89
  307.5 8.7 %convolution_bitcast_fusion = f32[8,4,6,1,4608]{4,0,2,1,3:T(8,128)S(1)} fusion(f32[8,4,8,4,1]{0,2,1,4,3:T(8,128)} %copy.24, f32[1,4,6,8,4608]{4,1,2,0,3:T(4,128)S(1)} %all-to-all-done), kind=kOutput, calls=%fused_computation.24 | convolution fusion | flops 339738624 | bytes 7081984 | tf_op jit(solution)/shard_map/iqxp,iqjo->joxp/dot_general | solution.py:90
  316.2 2.3 copy.22
  318.5 27.1 %all_to_all.30 = f32[8,4,6,1,4608]{4,1,3,2,0:T(4,128)S(1)} all-to-all(f32[8,4,6,1,4608]{4,1,3,2,0:T(4,128)S(1)} %copy.22), channel_id=1, replica_groups=mesh['domain'=32,'band'=8] {'band'}, dimensions={0} | all-to-all | bytes 7077888 | tf_op jit(solution)/shard_map/all_to_all | solution.py:91
  345.6 2.1 copy.23
  347.7 3.6 %reshape_squeeze.3 = f32[4,6,36864]{2,0,1:T(4,128)} reshape(f32[1,4,6,8,1,4608]{5,3,1,2,4,0:T(8,128)S(1)} %copy.23) | data formatting | bytes 7077888 | tf_op jit(solution)/shard_map/reshape;squeeze | solution.py:92
  (38 shorter events, 5.0 us)
Async XLA Ops:
  3.4 55.3 %copy-start = (f32[4,6,36864]{2,0,1:T(4,128)S(1)}, f32[4,6,36864]{2,0,1:T(4,128)}, u32[]{:S(2)}) copy-start(f32[4,6,36864]{2,0,1:T(4,128)} %param.4) | copy-start | bytes 10616836
  3.4 55.1 %collective-permute-start.1 = (f32[4,4,36864]{2,0,1:T(4,128)S(1)}, f32[4,4,36864]{2,0,1:T(4,128)S(1)}, u32[]{:S(2)}, u32[]{:S(2)}) collective-permute-start(f32[4,4,36864]{2,0,1:T(4,128)S(1)} %get-tuple-element.11), channel_id=1, source_target_pairs={{0,8},{8,16},{16,24},{24,32},{32,40},{40,48},{48,56},{56,64},{64,7... | collective-permute-start | bytes 7077896 | tf_op jit(solution)/shard_map/ppermute | solution.py:20
  3.5 56.4 %collective-permute-start = (f32[4,4,36864]{2,0,1:T(4,128)S(1)}, f32[4,4,36864]{2,0,1:T(4,128)S(1)}, u32[]{:S(2)}, u32[]{:S(2)}) collective-permute-start(f32[4,4,36864]{2,0,1:T(4,128)S(1)} %get-tuple-element.10), channel_id=1, source_target_pairs={{8,0},{16,8},{24,16},{32,24},{40,32},{48,40},{56,48},{64,56},{72,6... | collective-permute-start | bytes 7077896 | tf_op jit(solution)/shard_map/ppermute | solution.py:21
  88.0 2.7 copy-start.2
  88.1 54.3 %copy-start.1 = (f32[4,6,36864]{2,0,1:T(4,128)S(1)}, f32[4,6,36864]{2,0,1:T(4,128)}, u32[]{:S(2)}) copy-start(f32[4,6,36864]{2,0,1:T(4,128)} %get-tuple-element.5) | copy-start | bytes 10616836
  88.1 54.3 %copy-start.3 = (f32[36864]{0:T(1024)S(1)}, f32[36864]{0:T(1024)}, u32[]{:S(2)}) copy-start(f32[36864]{0:T(1024)} %get-tuple-element.19) | copy-start | bytes 442372
  88.1 54.3 %copy-start.4 = (f32[36864]{0:T(1024)S(1)}, f32[36864]{0:T(1024)}, u32[]{:S(2)}) copy-start(f32[36864]{0:T(1024)} %get-tuple-element.20) | copy-start | bytes 442372
  88.1 54.3 %copy-start.5 = (f32[36864]{0:T(1024)S(1)}, f32[36864]{0:T(1024)}, u32[]{:S(2)}) copy-start(f32[36864]{0:T(1024)} %get-tuple-element.21) | copy-start | bytes 442372
  88.1 54.3 %copy-start.6 = (f32[36864]{0:T(1024)S(1)}, f32[36864]{0:T(1024)}, u32[]{:S(2)}) copy-start(f32[36864]{0:T(1024)} %get-tuple-element.22) | copy-start | bytes 442372
  88.1 54.3 %copy-start.7 = (f32[36864]{0:T(1024)S(1)}, f32[36864]{0:T(1024)}, u32[]{:S(2)}) copy-start(f32[36864]{0:T(1024)} %get-tuple-element.23) | copy-start | bytes 442372
  88.7 53.6 %collective-permute-start.2 = (f32[4,4,36864]{2,0,1:T(4,128)S(1)}, f32[4,4,36864]{2,0,1:T(4,128)S(1)}, u32[]{:S(2)}, u32[]{:S(2)}) collective-permute-start(f32[4,4,36864]{2,0,1:T(4,128)S(1)} %get-tuple-element.8), channel_id=1, source_target_pairs={{8,0},{16,8},{24,16},{32,24},{40,32},{48,40},{56,48},{64,56},{72,6... | collective-permute-start | bytes 7077896 | tf_op jit(solution)/shard_map/ppermute | solution.py:21
  90.7 51.6 %collective-permute-start.3 = (f32[4,4,36864]{2,0,1:T(4,128)S(1)}, f32[4,4,36864]{2,0,1:T(4,128)S(1)}, u32[]{:S(2)}, u32[]{:S(2)}) collective-permute-start(f32[4,4,36864]{2,0,1:T(4,128)S(1)} %get-tuple-element.9), channel_id=1, source_target_pairs={{0,8},{8,16},{16,24},{24,32},{32,40},{40,48},{48,56},{56,64},{64,7... | collective-permute-start | bytes 7077896 | tf_op jit(solution)/shard_map/ppermute | solution.py:20
  169.6 54.9 %collective-permute-start.4 = (f32[4,4,36864]{2,0,1:T(4,128)S(1)}, f32[4,4,36864]{2,0,1:T(4,128)S(1)}, u32[]{:S(2)}, u32[]{:S(2)}) collective-permute-start(f32[4,4,36864]{2,0,1:T(4,128)S(1)} %get-tuple-element.6), channel_id=1, source_target_pairs={{8,0},{16,8},{24,16},{32,24},{40,32},{48,40},{56,48},{64,56},{72,6... | collective-permute-start | bytes 7077896 | tf_op jit(solution)/shard_map/ppermute | solution.py:21
  173.1 51.4 %collective-permute-start.5 = (f32[4,4,36864]{2,0,1:T(4,128)S(1)}, f32[4,4,36864]{2,0,1:T(4,128)S(1)}, u32[]{:S(2)}, u32[]{:S(2)}) collective-permute-start(f32[4,4,36864]{2,0,1:T(4,128)S(1)} %get-tuple-element.7), channel_id=1, source_target_pairs={{0,8},{8,16},{16,24},{24,32},{32,40},{40,48},{48,56},{56,64},{64,7... | collective-permute-start | bytes 7077896 | tf_op jit(solution)/shard_map/ppermute | solution.py:20
  261.9 5.4 %copy-start.8 = (s32[2]{0:T(128)S(1)}, s32[2]{0:T(128)}, u32[]{:S(2)}) copy-start(s32[2]{0:T(128)} %param.7) | copy-start | bytes 28
  261.9 45.7 %all-to-all-start = ((f32[1,4,6,8,4608]{4,1,2,0,3:T(4,128)}), f32[1,4,6,8,4608]{4,1,2,0,3:T(4,128)S(1)}, u32[]{:S(2)}, u32[]{:S(2)}) async-start(f32[1,4,6,8,4608]{4,1,2,0,3:T(4,128)} %copy.19), calls=%async_computation | async-start | bytes 7077888 | tf_op jit(solution)/shard_map/all_to_all | solution.py:89

commit v2 on v0

v2 whole, which is shorter than its diff:
```python
import functools

import jax
import jax.numpy as jnp
import numpy as np
from jax import lax
from jax.experimental import pallas as pl
from jax.experimental.pallas import tpu as pltpu
from jax.sharding import PartitionSpec as P


NZ = 192
lap_coeffs = (-205.0 / 72.0, 8.0 / 5.0, -1.0 / 5.0, 8.0 / 315.0, -1.0 / 560.0)
weights = tuple(-0.1 * value for value in lap_coeffs)


def along_z():
    cell = lax.broadcasted_iota(jnp.int32, (384, 384), 0)
    other = lax.broadcasted_iota(jnp.int32, (384, 384), 1)
    apart = jnp.abs(cell - other)
    same = (cell < NZ) == (other < NZ)
    parts = [jnp.zeros((384, 384), jnp.bfloat16)] * 2
    for k in range(1, 5):
        rounded = np.float32(weights[k]).astype(jnp.bfloat16)
        rest = np.float32(weights[k] - float(rounded)).astype(jnp.bfloat16)
        parts = [jnp.where((apart == k) & same, value, part) for value, part in zip((rounded, rest), parts)]
    return jnp.concatenate([parts[0], parts[0], parts[1]], axis=0)


def inner_kernel(own, scaled, line, *rest, group, first):
    if first:
        out, field, half, even, odd = rest
        before = None
    else:
        before, out, field, half, even, odd = rest
    planes, rows, _ = own.shape
    pad = 24 * group
    step = 3 * group
    blocks = rows // pad
    zeros = jnp.zeros((pad, 128), jnp.float32)
    left = lax.broadcasted_iota(jnp.int32, (8, 128), 1) < 64

    def strided(ref, x, at):
        return ref[x, pl.ds(at, 8, stride=step), :]

    for x in range(planes):
        field[x, 0:pad] = zeros
        field[x, pad + rows :] = zeros
        half[x, pad + rows :] = zeros

    def fill(i, carry):
        at = pl.multiple_of(i * pad, 8)
        for x in range(planes):
            field[x, pl.ds(pad + at, pad), :] = own[x, pl.ds(at, pad), :]
        return carry

    lax.fori_loop(0, blocks, fill, 0)

    def halve(i, carry):
        for x in range(planes):
            for o in range(group):
                tiles = [strided(field, x, i * pad + a * group + o) for a in range(4)]
                for a in range(3):
                    turned = pltpu.roll(jnp.where(left, tiles[a + 1], tiles[a]), 64, 1)
                    half[x, pl.ds(i * pad + a * group + o, 8, stride=step), :] = turned
        return carry

    lax.fori_loop(0, blocks + 1, halve, 0)

    def multiply(i):
        pieces = [
            jnp.concatenate(
                [strided(own, x, i * pad + a * group + o) for x in range(planes) for o in range(group)],
                axis=0,
            )
            for a in range(3)
        ]
        exact = jnp.concatenate(pieces, axis=1)
        high_part = exact.astype(jnp.bfloat16)
        low_part = (exact - high_part.astype(jnp.float32)).astype(jnp.bfloat16)
        return jnp.dot(
            jnp.concatenate([high_part, low_part, high_part], axis=1),
            line[...],
            preferred_element_type=jnp.float32,
        )

    def compute(i, part):
        for o in range(group):
            for a in range(3):
                at = i * pad + a * group + o
                column = [strided(own, x, at) for x in range(planes)]
                for x in range(planes):

                    def near(ref, tiles):
                        return strided(ref, x, pad + at + tiles * group)

                    row = (x * group + o) * 8
                    total = part[row : row + 8, 128 * a : 128 * a + 128]
                    total = total + scaled[x, pl.ds(i * 24 + a, 8, stride=3), :] * column[x]
                    pairs = (
                        near(half, 1) + near(half, -2),
                        near(field, 3) + near(field, -3),
                        near(half, 4) + near(half, -5),
                        near(field, 6) + near(field, -6),
                    )
                    for k in range(1, 5):
                        around = pairs[k - 1]
                        if x - k >= 0:
                            around = around + column[x - k]
                        if x + k < planes:
                            around = around + column[x + k]
                        total = total + weights[k] * around
                    if not first:
                        total = 2.0 * total - strided(before, x, at)
                    out[x, pl.ds(at, 8, stride=step), :] = total

    even[...] = multiply(0)

    def pair(i, carry):
        odd[...] = multiply(2 * i + 1)
        compute(2 * i, even)
        even[...] = multiply(jnp.minimum(2 * i + 2, blocks - 1))
        compute(2 * i + 1, odd)
        return carry

    lax.fori_loop(0, blocks // 2, pair, 0)


def inner(own, scaled, line, before, group):
    planes, rows, _ = own.shape
    first = before is None
    operands = (own, scaled, line) + (() if first else (before,))
    padded = (planes, rows + 48 * group, 128)
    return pl.pallas_call(
        functools.partial(inner_kernel, group=group, first=first),
        out_shape=jax.ShapeDtypeStruct(own.shape, jnp.float32),
        in_specs=[pl.BlockSpec(memory_space=pltpu.VMEM)] * len(operands),
        out_specs=pl.BlockSpec(memory_space=pltpu.VMEM),
        scratch_shapes=[
            pltpu.VMEM(padded, jnp.float32),
            pltpu.VMEM(padded, jnp.float32),
            pltpu.VMEM((planes * group * 8, 384), jnp.float32),
            pltpu.VMEM((planes * group * 8, 384), jnp.float32),
        ],
        name="inner_first" if first else "inner_next",
    )(*operands)


def edge_kernel(partial, low, top, out, *, factor):
    rows = partial.shape[1]

    def add(halo, nearby):
        def body(i, carry):
            at = pl.ds(pl.multiple_of(i * 8, 8), 8)
            beyond = [halo[x, at, :] for x in range(4)]
            for x in range(4):
                total = partial[x, at, :]
                for k in range(1, 5):
                    if nearby(x, k) is not None:
                        total = total + (factor * weights[k]) * beyond[nearby(x, k)]
                out[x, at, :] = total
            return carry

        lax.fori_loop(0, rows // 8, body, 0, unroll=4)

    @pl.when(pl.program_id(0) == 0)
    def _():
        add(low, lambda x, k: 4 + x - k if x < k else None)

    @pl.when(pl.program_id(0) == 1)
    def _():
        add(top, lambda x, k: x + k - 4 if x + k > 3 else None)


def edges(partial, low, top, factor):
    planes, rows, _ = partial.shape
    end = pl.BlockSpec((4, rows, 128), lambda i: (i * (planes // 4 - 1), 0, 0))
    halo = pl.BlockSpec((4, rows, 128), lambda i: (0, 0, 0))
    return pl.pallas_call(
        functools.partial(edge_kernel, factor=factor),
        grid=(2,),
        out_shape=jax.ShapeDtypeStruct(partial.shape, jnp.float32),
        in_specs=[end, halo, halo],
        out_specs=end,
        input_output_aliases={0: 0},
        name="edges",
    )(partial, low, top)


def rotate_kernel(source, mixing, field, out):
    bands, rows, _ = field.shape
    step = 8

    def body(i, carry):
        base = i * (step * 4)

        def orbital(band, q):
            return field[band, pl.ds(base + q, step, stride=4), :]

        shared = [orbital(source[t], q) for t in range(2) for q in range(4)]
        for band in range(bands):
            own = [orbital(band, q) for q in range(4)]
            for o in range(4):
                total = mixing[0, band, 0, o] * own[0]
                for q in range(1, 4):
                    total = total + mixing[0, band, q, o] * own[q]
                for t in range(2):
                    for q in range(4):
                        total = total + mixing[1 + t, band, q, o] * shared[4 * t + q]
                out[band, pl.ds(base + o, step, stride=4), :] = total
        return carry

    lax.fori_loop(0, rows // (step * 4), body, 0)


def rotate(source, mixing, field):
    return pl.pallas_call(
        rotate_kernel,
        out_shape=jax.ShapeDtypeStruct(field.shape, jnp.float32),
        in_specs=[
            pl.BlockSpec(memory_space=pltpu.SMEM),
            pl.BlockSpec(memory_space=pltpu.SMEM),
            pl.BlockSpec(memory_space=pltpu.VMEM),
        ],
        out_specs=pl.BlockSpec(memory_space=pltpu.VMEM),
        name="rotate",
    )(source, mixing, field)


AXES = ("domain", "band")


def split_kernel(orbit, rows, *outs):
    tiles = outs[0].shape[1]

    def body(i, carry):
        at = pl.ds(pl.multiple_of(i * 8, 8), 8)
        for k, out in enumerate(outs):
            out[0, at, :] = rows[0, pl.ds(i * 32 + orbit[k], 8, stride=4), :]
        return carry

    lax.fori_loop(0, tiles // 8, body, 0, unroll=4)


def split(orbit, rows):
    planes, count, _ = rows.shape
    small = pl.BlockSpec((1, count // 4, 128), lambda x: (x, 0, 0))
    return pl.pallas_call(
        split_kernel,
        grid=(planes,),
        out_shape=[jax.ShapeDtypeStruct((planes, count // 4, 128), jnp.float32)] * 4,
        in_specs=[pl.BlockSpec(memory_space=pltpu.SMEM), pl.BlockSpec((1, count, 128), lambda x: (x, 0, 0))],
        out_specs=[small] * 4,
        name="split",
    )(orbit, rows)


def merge_kernel(orbit, *refs):
    out = refs[-1]
    tiles = refs[0].shape[1]

    def body(i, carry):
        at = pl.ds(pl.multiple_of(i * 8, 8), 8)
        for k, part in enumerate(refs[:-1]):
            out[0, pl.ds(i * 32 + orbit[k], 8, stride=4), :] = part[0, at, :]
        return carry

    lax.fori_loop(0, tiles // 8, body, 0, unroll=4)


def merge(orbit, parts):
    planes, tiles, _ = parts[0].shape
    small = pl.BlockSpec((1, tiles, 128), lambda x: (x, 0, 0))
    return pl.pallas_call(
        merge_kernel,
        grid=(planes,),
        out_shape=jax.ShapeDtypeStruct((planes, tiles * 4, 128), jnp.float32),
        in_specs=[pl.BlockSpec(memory_space=pltpu.SMEM)] + [small] * 4,
        out_specs=pl.BlockSpec((1, tiles * 4, 128), lambda x: (x, 0, 0)),
        name="merge",
    )(orbit, *parts)


def place_kernel(slot, *refs):
    out, sems = refs[-2], refs[-1]
    planes = refs[0].shape[0]
    copies = [
        pltpu.make_async_copy(part, out.at[pl.ds(slot[k] * planes, planes)], sems.at[k])
        for k, part in enumerate(refs[:-2])
    ]
    for copy in copies:
        copy.start()
    for copy in copies:
        copy.wait()


def place(slot, parts):
    planes, tiles, _ = parts[0].shape
    return pl.pallas_call(
        place_kernel,
        out_shape=jax.ShapeDtypeStruct((planes * 4, tiles, 128), jnp.float32),
        in_specs=[pl.BlockSpec(memory_space=pltpu.SMEM)] + [pl.BlockSpec(memory_space=pl.ANY)] * 4,
        out_specs=pl.BlockSpec(memory_space=pltpu.VMEM),
        scratch_shapes=[pltpu.SemaphoreType.DMA((4,))],
        name="place",
    )(slot, *parts)


def route(move):
    def at(x, y, z, c):
        return (z * 4 + y // 2 * 2 + c) * 8 + x * 2 + y % 2

    pairs = []
    for z in range(8):
        for y in range(4):
            for c in range(2):
                for x in range(4):
                    to_x, to_y, to_z, to_c = move(x, y, z, c)
                    pairs.append((at(x, y, z, c), at(to_x % 4, to_y % 4, to_z % 8, to_c % 2)))
    return pairs


def send(value, move):
    return lax.ppermute(value, AXES, route(move))


STEPS = ((1, 0), (1, 1), (-1, 0), (-1, 1))
ORBIT = np.array(
    [[[(y + dy) % 4 // 2 * 2 + (c + dc) % 2 for dy, dc in STEPS] for c in range(2)] for y in range(4)],
    np.int32,
)
SLOT = np.array(
    [[[(y - dy) % 4 // 2 * 2 + (c + dc) % 2 for dy, dc in STEPS] for c in range(2)] for y in range(4)],
    np.int32,
)


def whole_potential(slab, chip_x, high, core):
    planes, tiles, _ = slab.shape
    part = planes * tiles // 4
    mine = lax.dynamic_slice_in_dim(slab.reshape(4 * part, 128), chip_x * part, part)
    there = send(mine, lambda x, y, z, c: (x, y + (1 if y % 2 else -1), z, c))
    pieces = [there] + [send(there, lambda x, y, z, c, k=k: (x + k, y, z, c)) for k in range(1, 4)]
    stacked = jnp.stack(pieces)
    other = jnp.concatenate([lax.dynamic_index_in_dim(stacked, (chip_x - k) % 4, 0, False) for k in range(4)])
    other = other.reshape(slab.shape)
    both = jnp.where(high == 0, jnp.stack([slab, other]), jnp.stack([other, slab]))
    across = send(both, lambda x, y, z, c: (x, y, z, c + 1))
    cores = jnp.where(core == 0, jnp.stack([both, across], 1), jnp.stack([across, both], 1))
    return cores.reshape(4 * planes, tiles, 128)


def to_rows(block):
    width, planes, cells = block.shape
    tiles = block.reshape(width, planes, cells // 128, 128)
    return tiles.transpose(1, 2, 0, 3).reshape(planes, cells // 128 * width, 128)


def from_rows(rows, width):
    planes, count, _ = rows.shape
    tiles = rows.reshape(planes, count // width, width, 128).transpose(2, 0, 1, 3)
    return tiles.reshape(width, planes, count // width * 128)


def mixing_weights(coefficients, owners, width, bands):
    cut = coefficients.reshape(bands, width, bands, width)
    own = jnp.stack([cut[band, :, band, :] for band in range(bands)])
    parts = [own]
    for turn in range(2):
        source, offset = owners[turn] // width, owners[turn] % width
        rows = lax.dynamic_slice(coefficients, (source * width, 0), (width, bands * width))
        rows = jnp.roll(rows, offset, axis=0)
        parts.append(rows.reshape(width, bands, width).transpose(1, 0, 2))
    return jnp.stack(parts)


def body(orbitals, potential, coefficients, owners):
    width, planes, cells = orbitals.shape
    bands = lax.axis_size("band")
    tiles = cells // 128
    place_d, place_b = lax.axis_index("domain"), lax.axis_index("band")
    core, high, chip_x = place_d % 2, place_d // 2 % 2, place_b // 2
    chip_y = high * 2 + place_b % 2
    orbit = jnp.asarray(ORBIT)[chip_y, core]
    slot = jnp.asarray(SLOT)[chip_y, core]

    parts = split(orbit, to_rows(orbitals))
    parts = [
        send(part, lambda x, y, z, c, dy=dy, dc=dc: (x, y + dy, z, c + dc))
        for part, (dy, dc) in zip(parts, STEPS)
    ]
    scaled = (potential - 6.0) * 0.2 - 0.3 * lap_coeffs[0]
    scaled = whole_potential(scaled.reshape(planes, tiles, 128), chip_x, high, core)
    line = along_z()
    previous, current = None, place(slot, parts)
    for factor in (1.0, 2.0, 2.0):
        low = send(current[-4:], lambda x, y, z, c: (x, y, z + 1, c))
        top = send(current[:4], lambda x, y, z, c: (x, y, z - 1, c))
        partial = inner(current, scaled, line, previous, 1)
        previous, current = current, edges(partial, low, top, factor)

    parts = [
        send(
            lax.dynamic_slice_in_dim(current, slot[k] * planes, planes),
            lambda x, y, z, c, dy=dy, dc=dc: (x, y - dy, z, c + dc),
        )
        for k, (dy, dc) in enumerate(STEPS)
    ]
    current = merge(orbit, parts)
    filtered = from_rows(current, width)
    gathered = lax.all_to_all(current.reshape(bands, planes, -1, 128), "band", 0, 0)
    mixing = mixing_weights(coefficients, owners, width, bands)
    turned = rotate(owners // width, mixing, gathered.reshape(bands, -1, 128))
    returned = lax.all_to_all(turned.reshape(bands, planes, -1, 128), "band", 0, 0)
    rotated = from_rows(returned.reshape(planes, tiles * width, 128), width)
    return (filtered, rotated)


def solution(mesh):
    in_specs = (P("band", "domain", None), P("domain", None), P(), P())
    out_specs = (P("band", "domain", None), P("band", "domain", None))
    return jax.shard_map(body, mesh=mesh, in_specs=in_specs, out_specs=out_specs, check_vma=False)
```

time: 614 us -> 328 us (0.53)
  waiting for transfers between devices: 432 us -> 124 us
  other arithmetic: 107 us -> 10.5 us
  Pallas kernels: 0 us -> 75.9 us
  blocking collectives: 0 us -> 45.1 us
  matrix products: 33 us -> 0 us
  starting transfers between devices: 8.78 us -> 32.6 us
  local copies, waits for them, and re-layouts: 10.3 us -> 28.3 us
  between operations: 18.2 us -> 8.82 us
    psum x1 -> x0, waiting for transfers between devices: 281 us -> none  [spread(): return lax.psum(kept, axis)]
    pallas_call x0 -> x10, Pallas kernels: none -> 75.9 us  [the longest x3 44.1 us: inner(): pl.pallas_call(functools.partial(inner_kernel, group=group, first=first),...]
    ppermute x6 -> x19, waiting for transfers between devices: 151 us -> 88.5 us  [send(): return lax.ppermute(value, AXES, route(move))]
    all_to_all x0 -> x1, blocking collectives: none -> 45.1 us  [body(): lax.all_to_all(turned.reshape(bands, planes, -1, 128), 'band', 0, 0)]
    select_n x3 -> x5, other arithmetic: 49 us -> 5.89 us  [the longest x1 2.11 us: whole_potential(): jnp.where(core == 0, jnp.stack([both, across], 1), jnp.stack([across, bot...]
    all_to_all x0 -> x1, waiting for transfers between devices: none -> 35.1 us  [body(): lax.all_to_all(current.reshape(bands, planes, -1, 128), 'band', 0, 0)]
    dot_general x3 -> x0, matrix products: 33 us -> none  [mixing(): jnp.einsum('bxp,bc->cxp', block, part_coeffs, precision=lax.Precision.HIG...]
    div x1 -> x0, other arithmetic: 28.5 us -> none  [chebyshev(): current = (hamiltonian(block, widen(block), potential) - 6.0 * block) / 5.0]
  transfers between devices with their start and end apart: 7 -> 20, of which waited for: 4 -> 10; matrix products, arithmetic and copies ran while one was open for 2% -> 6% of each run, Pallas kernels for 0% -> 17%
where the time goes in v2:
time: 328 us; the launch traced here: 325 us
  waiting for transfers between devices  124 us (38%)
  Pallas kernels  75.9 us (23%)
  blocking collectives  45.1 us (14%)
  starting transfers between devices  32.6 us (10%)
  local copies, waits for them, and re-layouts  28.3 us (9%)
  other arithmetic  10.5 us (3%)
  between operations  8.82 us (3%)
    ppermute x19, waiting for transfers between devices, send(): return lax.ppermute(value, AXES, route(move))  88.5 us
    all_to_all x1, blocking collectives, body(): lax.all_to_all(turned.reshape(bands, planes, -1, 128), 'band', 0, 0)  45.1 us
    pallas_call x3, Pallas kernels, inner(): pl.pallas_call(functools.partial(inner_kernel, group=group, first=first),...  44.1 us
    all_to_all x1, waiting for transfers between devices, body(): lax.all_to_all(current.reshape(bands, planes, -1, 128), 'band', 0, 0)  35.1 us
    ppermute x19, starting transfers between devices, send(): return lax.ppermute(value, AXES, route(move))  28.1 us
    pallas_call x1, Pallas kernels, rotate(): pl.pallas_call(rotate_kernel, out_shape=jax.ShapeDtypeStruct(field.shape,...  8.04 us
    pallas_call x3, Pallas kernels, edges(): pl.pallas_call(functools.partial(edge_kernel, factor=factor), grid=(2,),...  7.83 us
  transfers between devices with their start and end apart: 20, of which 10 were waited for; matrix products, arithmetic and copies ran while one was open for 6% of the time, Pallas kernels for 17%

profile of v2, /device:TPU:16, one launch (start us, length us, event | category | flops | bytes accessed | tf_op | source)
XLA Modules:
  0.0 324.8 jit_solution(16610384484476954226)
XLA Ops:
  3.2 6.7 %collective-permute-done.4 = f32[432,128]{1,0:T(8,128)S(1)} collective-permute-done((f32[432,128]{1,0:T(8,128)S(1)}, f32[432,128]{1,0:T(8,128)S(1)}, u32[]{:S(2)}, u32[]{:S(2)}) %collective-permute-start.4) | collective-permute-done | bytes 221216 | tf_op jit(solution)/shard_map/ppermute | solution.py:324
  11.4 2.7 collective-permute-start.6
  15.8 2.7 collective-permute-done.5
  18.4 4.7 %collective-permute-done.6 = f32[432,128]{1,0:T(8,128)S(1)} collective-permute-done((f32[432,128]{1,0:T(8,128)S(1)}, f32[432,128]{1,0:T(8,128)S(1)}, u32[]{:S(2)}, u32[]{:S(2)}) %collective-permute-start.6) | collective-permute-done | bytes 221216 | tf_op jit(solution)/shard_map/ppermute | solution.py:324
  26.0 5.7 %split.1 = (f32[6,288,128]{2,1,0:T(8,128)}, f32[6,288,128]{2,1,0:T(8,128)}, f32[6,288,128]{2,1,0:T(8,128)}, f32[6,288,128]{2,1,0:T(8,128)}) custom-call(s32[4]{0:T(128)} %fusion.12.orbit, f32[6,1152,128]{2,1,0:T(8,128)} %bitcast.84), custom_call_target="tpu_custom_call" | custom-call | tf_op jit(solution)/shard_map/split/pallas_call | solution.py:248
  38.3 16.2 %collective-permute-done.refs_0_ = f32[6,288,128]{2,1,0:T(8,128)} collective-permute-done((f32[6,288,128]{2,1,0:T(8,128)}, f32[6,288,128]{2,1,0:T(8,128)}, u32[]{:S(2)}, u32[]{:S(2)}) %collective-permute-start) | collective-permute-done | bytes 884768 | tf_op jit(solution)/shard_map/ppermute | solution.py:324
  54.5 18.5 %collective-permute-done.1.refs_1_ = f32[6,288,128]{2,1,0:T(8,128)} collective-permute-done((f32[6,288,128]{2,1,0:T(8,128)}, f32[6,288,128]{2,1,0:T(8,128)}, u32[]{:S(2)}, u32[]{:S(2)}) %collective-permute-start.1) | collective-permute-done | bytes 884768 | tf_op jit(solution)/shard_map/ppermute | solution.py:324
  74.8 4.5 %place.1.own.rest_0_ = f32[24,288,128]{2,1,0:T(8,128)} custom-call(s32[4]{0:T(128)} %fusion.20.slot, f32[6,288,128]{2,1,0:T(8,128)} %collective-permute-done.refs_0_, f32[6,288,128]{2,1,0:T(8,128)} %collective-permute-done.1.refs_1_, f32[6,288,128]{2,1,0:T(8,128)} %collective-permute-done.2.refs_2_, f32[6,288,128]{2,1,0:T(8,128)} %collective-permute-done.3.refs_3_), custom_call_target="tpu_custom_call" | custom-call | tf_op jit(solution)/shard_map/place/pallas_call | solution.py:299
  81.7 5.9 %collective-permute-start.10 = (f32[4,288,128]{2,1,0:T(8,128)}, f32[4,288,128]{2,1,0:T(8,128)}, u32[]{:S(2)}, u32[]{:S(2)}) collective-permute-start(f32[4,288,128]{2,1,0:T(8,128)} %get-tuple-element.19), channel_id=1, source_target_pairs={{0,224},{2,226},{4,228},{6,230},{8,232},{10,234},{12,236},{14,238}... | collective-permute-start | bytes 1769480 | tf_op jit(solution)/shard_map/ppermute | solution.py:324
  90.9 13.6 %inner_first.1.partial = f32[24,288,128]{2,1,0:T(8,128)} custom-call(f32[24,288,128]{2,1,0:T(8,128)} %place.1.own.rest_0_, f32[24,288,128]{2,1,0:T(8,128)} %bitcast.72, bf16[1152,384]{1,0:T(8,128)(2,1)} %pad_maximum_fusion.2.line), custom_call_target="tpu_custom_call" | custom-call | tf_op jit(solution)/shard_map/inner_first/pallas_call | solution.py:134
  104.6 2.6 edges.3.own.rest_0_
  108.8 3.3 %collective-permute-start.12 = (f32[4,288,128]{2,1,0:T(8,128)S(1)}, f32[4,288,128]{2,1,0:T(8,128)S(1)}, u32[]{:S(2)}, u32[]{:S(2)}) collective-permute-start(f32[4,288,128]{2,1,0:T(8,128)S(1)} %get-tuple-element.17), channel_id=1, source_target_pairs={{0,224},{2,226},{4,228},{6,230},{8,232},{10,234},{12,236},{14,238}... | collective-permute-start | bytes 1769480 | tf_op jit(solution)/shard_map/ppermute | solution.py:324
  112.1 15.2 %inner_next.2.partial = f32[24,288,128]{2,1,0:T(8,128)} custom-call(f32[24,288,128]{2,1,0:T(8,128)} %edges.3.own.rest_0_, f32[24,288,128]{2,1,0:T(8,128)} %bitcast.73, bf16[1152,384]{1,0:T(8,128)(2,1)} %pad_maximum_fusion.2.line, f32[24,288,128]{2,1,0:T(8,128)} %place.1.own.rest_0_), custom_call_target="tpu_custom_call" | custom-call | tf_op jit(solution)/shard_map/inner_next/pallas_call | solution.py:134
  133.1 3.2 collective-permute-start.14
  140.2 15.2 %inner_next.3.partial = f32[24,288,128]{2,1,0:T(8,128)} custom-call(f32[24,288,128]{2,1,0:T(8,128)} %edges.4.own, f32[24,288,128]{2,1,0:T(8,128)} %bitcast.74, bf16[1152,384]{1,0:T(8,128)(2,1)} %pad_maximum_fusion.2.line, f32[24,288,128]{2,1,0:T(8,128)} %edges.3.own.rest_0_), custom_call_target="tpu_custom_call" | custom-call | tf_op jit(solution)/shard_map/inner_next/pallas_call | solution.py:134
  166.6 17.8 %collective-permute-done.15.refs_0_ = f32[6,288,128]{2,1,0:T(8,128)S(1)} collective-permute-done((f32[6,288,128]{2,1,0:T(8,128)S(1)}, f32[6,288,128]{2,1,0:T(8,128)S(1)}, u32[]{:S(2)}, u32[]{:S(2)}) %collective-permute-start.15) | collective-permute-done | bytes 884768 | tf_op jit(solution)/shard_map/ppermute | solution.py:324
  184.4 16.3 %collective-permute-done.16.refs_1_ = f32[6,288,128]{2,1,0:T(8,128)S(1)} collective-permute-done((f32[6,288,128]{2,1,0:T(8,128)S(1)}, f32[6,288,128]{2,1,0:T(8,128)S(1)}, u32[]{:S(2)}, u32[]{:S(2)}) %collective-permute-start.16) | collective-permute-done | bytes 884768 | tf_op jit(solution)/shard_map/ppermute | solution.py:324
  200.7 3.8 %collective-permute-done.18.refs_3_ = f32[6,288,128]{2,1,0:T(8,128)S(1)} collective-permute-done((f32[6,288,128]{2,1,0:T(8,128)S(1)}, f32[6,288,128]{2,1,0:T(8,128)S(1)}, u32[]{:S(2)}, u32[]{:S(2)}) %collective-permute-start.18) | collective-permute-done | bytes 884768 | tf_op jit(solution)/shard_map/ppermute | solution.py:324
  205.4 5.8 %merge.1 = f32[6,1152,128]{2,1,0:T(8,128)} custom-call(s32[4]{0:T(128)} %fusion.12.orbit, f32[6,288,128]{2,1,0:T(8,128)} %copy-done.3, f32[6,288,128]{2,1,0:T(8,128)} %copy-done.4, f32[6,288,128]{2,1,0:T(8,128)} %copy-done.5, f32[6,288,128]{2,1,0:T(8,128)} %copy-done.6), custom_call_target="tpu_custom_call" | custom-call | tf_op jit(solution)/shard_map/merge/pallas_call | solution.py:274
  211.2 4.5 %all-to-all-start = ((f32[8,6,144,128]{3,2,1,0:T(8,128)}), f32[8,6,144,128]{3,2,1,0:T(8,128)S(1)}, u32[]{:S(2)}, u32[]{:S(2)}) async-start(f32[8,6,144,128]{3,2,1,0:T(8,128)} %bitcast.75), calls=%async_computation | async-start | bytes 7077888 | tf_op jit(solution)/shard_map/all_to_all | solution.py:411
  231.3 35.1 %all-to-all-done = f32[8,6,144,128]{3,2,1,0:T(8,128)S(1)} async-done(((f32[8,6,144,128]{3,2,1,0:T(8,128)}), f32[8,6,144,128]{3,2,1,0:T(8,128)S(1)}, u32[]{:S(2)}, u32[]{:S(2)}) %all-to-all-start) | async-done | bytes 3538976 | tf_op jit(solution)/shard_map/all_to_all | solution.py:411
  268.1 8.0 %rotate.1 = f32[8,864,128]{2,1,0:T(8,128)} custom-call(s32[2]{0:T(128)} %and_select_fusion.source, f32[3,8,4,4]{3,2,1,0:T(4,128)} %pad_maximum_fusion.3.mixing, f32[8,864,128]{2,1,0:T(8,128)} %bitcast.77), custom_call_target="tpu_custom_call" | custom-call | tf_op jit(solution)/shard_map/rotate/pallas_call | solution.py:217
  276.2 45.1 %all_to_all.10 = f32[8,6,144,128]{3,2,1,0:T(8,128)S(1)} all-to-all(f32[8,6,144,128]{3,2,1,0:T(8,128)} %bitcast.78), channel_id=1, replica_groups=mesh['domain'=32,'band'=8] {'band'}, dimensions={0} | all-to-all | bytes 7077888 | tf_op jit(solution)/shard_map/all_to_all | solution.py:414
  321.7 3.1 reshape.127
  (95 shorter events, 55.7 us)
Async XLA Ops:
  2.7 7.3 %collective-permute-start.4 = (f32[432,128]{1,0:T(8,128)S(1)}, f32[432,128]{1,0:T(8,128)S(1)}, u32[]{:S(2)}, u32[]{:S(2)}) collective-permute-start(f32[432,128]{1,0:T(8,128)S(1)} %constant_dynamic-slice_fusion.8), channel_id=1, source_target_pairs={{0,17},{2,19},{4,21},{6,23},{8,25},{10,27},{12,29},{14,31},{1,16},... | collective-permute-start | bytes 663560 | tf_op jit(solution)/shard_map/ppermute | solution.py:324
  9.9 8.5 %collective-permute-start.5 = (f32[432,128]{1,0:T(8,128)S(1)}, f32[432,128]{1,0:T(8,128)S(1)}, u32[]{:S(2)}, u32[]{:S(2)}) collective-permute-start(f32[432,128]{1,0:T(8,128)S(1)} %collective-permute-done.4), channel_id=1, source_target_pairs={{0,2},{2,4},{4,6},{6,0},{8,10},{10,12},{12,14},{14,8},{1,3},{3,5},... | collective-permute-start | bytes 663560 | tf_op jit(solution)/shard_map/ppermute | solution.py:324
  11.4 11.8 %collective-permute-start.6 = (f32[432,128]{1,0:T(8,128)S(1)}, f32[432,128]{1,0:T(8,128)S(1)}, u32[]{:S(2)}, u32[]{:S(2)}) collective-permute-start(f32[432,128]{1,0:T(8,128)S(1)} %collective-permute-done.4), channel_id=1, source_target_pairs={{0,4},{2,6},{4,0},{6,2},{8,12},{10,14},{12,8},{14,10},{1,5},{3,7},... | collective-permute-start | bytes 663560 | tf_op jit(solution)/shard_map/ppermute | solution.py:324
  14.1 9.0 %collective-permute-start.7 = (f32[432,128]{1,0:T(8,128)S(1)}, f32[432,128]{1,0:T(8,128)S(1)}, u32[]{:S(2)}, u32[]{:S(2)}) collective-permute-start(f32[432,128]{1,0:T(8,128)S(1)} %collective-permute-done.4), channel_id=1, source_target_pairs={{0,6},{2,0},{4,2},{6,4},{8,14},{10,8},{12,10},{14,12},{1,7},{3,1},... | collective-permute-start | bytes 663560 | tf_op jit(solution)/shard_map/ppermute | solution.py:324
  24.7 64.1 %collective-permute-start.8 = (f32[2,6,288,128]{3,2,1,0:T(8,128)}, f32[2,6,288,128]{3,2,1,0:T(8,128)S(1)}, u32[]{:S(2)}, u32[]{:S(2)}) collective-permute-start(f32[2,6,288,128]{3,2,1,0:T(8,128)} %maximum_select_fusion.2), channel_id=1, source_target_pairs={{0,8},{2,10},{4,12},{6,14},{8,0},{10,2},{12,4},{14,6},{1,9},{3,11}... | collective-permute-start | bytes 5308424 | tf_op jit(solution)/shard_map/ppermute | solution.py:324
  31.7 22.8 %collective-permute-start = (f32[6,288,128]{2,1,0:T(8,128)}, f32[6,288,128]{2,1,0:T(8,128)}, u32[]{:S(2)}, u32[]{:S(2)}) collective-permute-start(f32[6,288,128]{2,1,0:T(8,128)} %get-tuple-element.7), channel_id=1, source_target_pairs={{0,1},{2,3},{4,5},{6,7},{8,9},{10,11},{12,13},{14,15},{1,16},{3,18... | collective-permute-start | bytes 2654216 | tf_op jit(solution)/shard_map/ppermute | solution.py:324
  34.2 38.9 %collective-permute-start.1 = (f32[6,288,128]{2,1,0:T(8,128)}, f32[6,288,128]{2,1,0:T(8,128)}, u32[]{:S(2)}, u32[]{:S(2)}) collective-permute-start(f32[6,288,128]{2,1,0:T(8,128)} %get-tuple-element.8), channel_id=1, source_target_pairs={{0,9},{2,11},{4,13},{6,15},{8,1},{10,3},{12,5},{14,7},{1,24},{3,26... | collective-permute-start | bytes 2654216 | tf_op jit(solution)/shard_map/ppermute | solution.py:324
  34.4 38.7 %collective-permute-start.2 = (f32[6,288,128]{2,1,0:T(8,128)}, f32[6,288,128]{2,1,0:T(8,128)}, u32[]{:S(2)}, u32[]{:S(2)}) collective-permute-start(f32[6,288,128]{2,1,0:T(8,128)} %get-tuple-element.9), channel_id=1, source_target_pairs={{0,17},{2,19},{4,21},{6,23},{8,25},{10,27},{12,29},{14,31},{1,0},{... | collective-permute-start | bytes 2654216 | tf_op jit(solution)/shard_map/ppermute | solution.py:324
  36.1 38.7 %collective-permute-start.3 = (f32[6,288,128]{2,1,0:T(8,128)}, f32[6,288,128]{2,1,0:T(8,128)}, u32[]{:S(2)}, u32[]{:S(2)}) collective-permute-start(f32[6,288,128]{2,1,0:T(8,128)} %get-tuple-element.10), channel_id=1, source_target_pairs={{0,25},{2,27},{4,29},{6,31},{8,17},{10,19},{12,21},{14,23},{1,8},{... | collective-permute-start | bytes 2654216 | tf_op jit(solution)/shard_map/ppermute | solution.py:324
  79.3 8.3 %copy-start.1 = (bf16[384,384]{1,0:T(8,128)(2,1)S(1)}, bf16[384,384]{1,0:T(8,128)(2,1)}, u32[]{:S(2)}) copy-start(bf16[384,384]{1,0:T(8,128)(2,1)} %get-tuple-element.45) | copy-start | bytes 884740
  79.3 8.3 %copy-start.2 = (bf16[384,384]{1,0:T(8,128)(2,1)S(1)}, bf16[384,384]{1,0:T(8,128)(2,1)}, u32[]{:S(2)}) copy-start(bf16[384,384]{1,0:T(8,128)(2,1)} %get-tuple-element.46) | copy-start | bytes 884740
  81.7 22.9 %collective-permute-start.10 = (f32[4,288,128]{2,1,0:T(8,128)}, f32[4,288,128]{2,1,0:T(8,128)}, u32[]{:S(2)}, u32[]{:S(2)}) collective-permute-start(f32[4,288,128]{2,1,0:T(8,128)} %get-tuple-element.19), channel_id=1, source_target_pairs={{0,224},{2,226},{4,228},{6,230},{8,232},{10,234},{12,236},{14,238}... | collective-permute-start | bytes 1769480 | tf_op jit(solution)/shard_map/ppermute | solution.py:324
  87.6 17.0 %collective-permute-start.9 = (f32[4,288,128]{2,1,0:T(8,128)}, f32[4,288,128]{2,1,0:T(8,128)}, u32[]{:S(2)}, u32[]{:S(2)}) collective-permute-start(f32[4,288,128]{2,1,0:T(8,128)} %get-tuple-element.20), channel_id=1, source_target_pairs={{0,32},{2,34},{4,36},{6,38},{8,40},{10,42},{12,44},{14,46},{1,33},... | collective-permute-start | bytes 1769480 | tf_op jit(solution)/shard_map/ppermute | solution.py:324
  108.5 18.8 %collective-permute-start.11 = (f32[4,288,128]{2,1,0:T(8,128)S(1)}, f32[4,288,128]{2,1,0:T(8,128)S(1)}, u32[]{:S(2)}, u32[]{:S(2)}) collective-permute-start(f32[4,288,128]{2,1,0:T(8,128)S(1)} %get-tuple-element.18), channel_id=1, source_target_pairs={{0,32},{2,34},{4,36},{6,38},{8,40},{10,42},{12,44},{14,46},{1,33},... | collective-permute-start | bytes 1769480 | tf_op jit(solution)/shard_map/ppermute | solution.py:324
  108.8 18.5 %collective-permute-start.12 = (f32[4,288,128]{2,1,0:T(8,128)S(1)}, f32[4,288,128]{2,1,0:T(8,128)S(1)}, u32[]{:S(2)}, u32[]{:S(2)}) collective-permute-start(f32[4,288,128]{2,1,0:T(8,128)S(1)} %get-tuple-element.17), channel_id=1, source_target_pairs={{0,224},{2,226},{4,228},{6,230},{8,232},{10,234},{12,236},{14,238}... | collective-permute-start | bytes 1769480 | tf_op jit(solution)/shard_map/ppermute | solution.py:324
  133.0 22.4 %collective-permute-start.13 = (f32[4,288,128]{2,1,0:T(8,128)S(1)}, f32[4,288,128]{2,1,0:T(8,128)S(1)}, u32[]{:S(2)}, u32[]{:S(2)}) collective-permute-start(f32[4,288,128]{2,1,0:T(8,128)S(1)} %get-tuple-element.16), channel_id=1, source_target_pairs={{0,32},{2,34},{4,36},{6,38},{8,40},{10,42},{12,44},{14,46},{1,33},... | collective-permute-start | bytes 1769480 | tf_op jit(solution)/shard_map/ppermute | solution.py:324
  133.1 22.3 %collective-permute-start.14 = (f32[4,288,128]{2,1,0:T(8,128)S(1)}, f32[4,288,128]{2,1,0:T(8,128)S(1)}, u32[]{:S(2)}, u32[]{:S(2)}) collective-permute-start(f32[4,288,128]{2,1,0:T(8,128)S(1)} %get-tuple-element.15), channel_id=1, source_target_pairs={{0,224},{2,226},{4,228},{6,230},{8,232},{10,234},{12,236},{14,238}... | collective-permute-start | bytes 1769480 | tf_op jit(solution)/shard_map/ppermute | solution.py:324
  161.8 22.6 %collective-permute-start.15 = (f32[6,288,128]{2,1,0:T(8,128)S(1)}, f32[6,288,128]{2,1,0:T(8,128)S(1)}, u32[]{:S(2)}, u32[]{:S(2)}) collective-permute-start(f32[6,288,128]{2,1,0:T(8,128)S(1)} %get-tuple-element.14), channel_id=1, source_target_pairs={{0,17},{2,19},{4,21},{6,23},{8,25},{10,27},{12,29},{14,31},{1,0},{... | collective-permute-start | bytes 2654216 | tf_op jit(solution)/shard_map/ppermute | solution.py:324
  163.6 37.1 %collective-permute-start.16 = (f32[6,288,128]{2,1,0:T(8,128)S(1)}, f32[6,288,128]{2,1,0:T(8,128)S(1)}, u32[]{:S(2)}, u32[]{:S(2)}) collective-permute-start(f32[6,288,128]{2,1,0:T(8,128)S(1)} %get-tuple-element.13), channel_id=1, source_target_pairs={{0,25},{2,27},{4,29},{6,31},{8,17},{10,19},{12,21},{14,23},{1,8},{... | collective-permute-start | bytes 2654216 | tf_op jit(solution)/shard_map/ppermute | solution.py:324
  163.6 37.1 %collective-permute-start.17 = (f32[6,288,128]{2,1,0:T(8,128)S(1)}, f32[6,288,128]{2,1,0:T(8,128)S(1)}, u32[]{:S(2)}, u32[]{:S(2)}) collective-permute-start(f32[6,288,128]{2,1,0:T(8,128)S(1)} %get-tuple-element.12), channel_id=1, source_target_pairs={{0,1},{2,3},{4,5},{6,7},{8,9},{10,11},{12,13},{14,15},{1,16},{3,18... | collective-permute-start | bytes 2654216 | tf_op jit(solution)/shard_map/ppermute | solution.py:324
  164.0 40.5 %collective-permute-start.18 = (f32[6,288,128]{2,1,0:T(8,128)S(1)}, f32[6,288,128]{2,1,0:T(8,128)S(1)}, u32[]{:S(2)}, u32[]{:S(2)}) collective-permute-start(f32[6,288,128]{2,1,0:T(8,128)S(1)} %get-tuple-element.11), channel_id=1, source_target_pairs={{0,9},{2,11},{4,13},{6,15},{8,1},{10,3},{12,5},{14,7},{1,24},{3,26... | collective-permute-start | bytes 2654216 | tf_op jit(solution)/shard_map/ppermute | solution.py:324
  184.4 20.1 %copy-start.3 = (f32[6,288,128]{2,1,0:T(8,128)}, f32[6,288,128]{2,1,0:T(8,128)S(1)}, u32[]{:S(2)}) copy-start(f32[6,288,128]{2,1,0:T(8,128)S(1)} %collective-permute-done.15.refs_0_) | copy-start | bytes 2654212
  211.2 11.3 %copy-start.11 = (f32[32,32]{1,0:T(8,128)S(1)}, f32[32,32]{1,0:T(8,128)}, u32[]{:S(2)}) copy-start(f32[32,32]{1,0:T(8,128)} %param.10) | copy-start | bytes 12292
  211.2 55.1 %all-to-all-start = ((f32[8,6,144,128]{3,2,1,0:T(8,128)}), f32[8,6,144,128]{3,2,1,0:T(8,128)S(1)}, u32[]{:S(2)}, u32[]{:S(2)}) async-start(f32[8,6,144,128]{3,2,1,0:T(8,128)} %bitcast.75), calls=%async_computation | async-start | bytes 7077888 | tf_op jit(solution)/shard_map/all_to_all | solution.py:411
  (8 other events, 13.6 us)

commit v3 on v2

--- a/solution.py
+++ b/solution.py
@@ -187,19 +187,20 @@
     )(partial, low, top)
 
 
-def rotate_kernel(source, mixing, field, out):
-    bands, rows, _ = field.shape
-    step = 8
+def rotate_kernel(picked, mixing, field, *outs):
+    bands = len(outs)
+    tiles = field.shape[1]
 
     def body(i, carry):
-        base = i * (step * 4)
-
-        def orbital(band, q):
-            return field[band, pl.ds(base + q, step, stride=4), :]
-
-        shared = [orbital(source[t], q) for t in range(2) for q in range(4)]
-        for band in range(bands):
-            own = [orbital(band, q) for q in range(4)]
+        at = pl.ds(pl.multiple_of(i * 8, 8), 8)
+
+        def members(band):
+            return [field[q * bands + band + 1 - 2 * (band % 2), at, :] for q in range(4)]
+
+        shared = members(picked[0]) + members(picked[1])
+        for k, out in enumerate(outs):
+            band = picked[2] ^ k
+            own = members(band)
             for o in range(4):
                 total = mixing[0, band, 0, o] * own[0]
                 for q in range(1, 4):
@@ -207,24 +208,26 @@
                 for t in range(2):
                     for q in range(4):
                         total = total + mixing[1 + t, band, q, o] * shared[4 * t + q]
-                out[band, pl.ds(base + o, step, stride=4), :] = total
-        return carry
-
-    lax.fori_loop(0, rows // (step * 4), body, 0)
-
-
-def rotate(source, mixing, field):
+                out[pl.ds(i * 32 + o, 8, stride=4), :] = total
+        return carry
+
+    lax.fori_loop(0, tiles // 8, body, 0)
+
+
+def rotate(picked, mixing, field):
+    count, tiles, _ = field.shape
+    bands = count // 4
     return pl.pallas_call(
         rotate_kernel,
-        out_shape=jax.ShapeDtypeStruct(field.shape, jnp.float32),
+        out_shape=[jax.ShapeDtypeStruct((tiles * 4, 128), jnp.float32)] * bands,
         in_specs=[
             pl.BlockSpec(memory_space=pltpu.SMEM),
             pl.BlockSpec(memory_space=pltpu.SMEM),
             pl.BlockSpec(memory_space=pltpu.VMEM),
         ],
-        out_specs=pl.BlockSpec(memory_space=pltpu.VMEM),
+        out_specs=[pl.BlockSpec(memory_space=pltpu.VMEM)] * bands,
         name="rotate",
-    )(source, mixing, field)
+    )(picked, mixing, field)
 
 
 AXES = ("domain", "band")
@@ -295,13 +298,13 @@
 
 
 def place(slot, parts):
-    planes, tiles, _ = parts[0].shape
+    count, first = len(parts), parts[0].shape
     return pl.pallas_call(
         place_kernel,
-        out_shape=jax.ShapeDtypeStruct((planes * 4, tiles, 128), jnp.float32),
-        in_specs=[pl.BlockSpec(memory_space=pltpu.SMEM)] + [pl.BlockSpec(memory_space=pl.ANY)] * 4,
+        out_shape=jax.ShapeDtypeStruct((first[0] * count, *first[1:]), jnp.float32),
+        in_specs=[pl.BlockSpec(memory_space=pltpu.SMEM)] + [pl.BlockSpec(memory_space=pl.ANY)] * count,
         out_specs=pl.BlockSpec(memory_space=pltpu.VMEM),
-        scratch_shapes=[pltpu.SemaphoreType.DMA((4,))],
+        scratch_shapes=[pltpu.SemaphoreType.DMA((count,))],
         name="place",
     )(slot, *parts)
 
@@ -399,6 +402,13 @@
         partial = inner(current, scaled, line, previous, 1)
         previous, current = current, edges(partial, low, top, factor)
 
+    layer = [[first + k for k in range(4 * bands)] for first in range(0, 32 * bands, 4 * bands)]
+    gathered = lax.all_to_all(
+        current.reshape(4 * bands, -1, 128), AXES, 0, 0, axis_index_groups=layer, tiled=True
+    )
+    mixing = mixing_weights(coefficients, owners, width, bands)
+    picked = jnp.concatenate([owners // width, place_b[None].astype(jnp.int32)])
+    turned = rotate(picked, mixing, gathered)
     parts = [
         send(
             lax.dynamic_slice_in_dim(current, slot[k] * planes, planes),
@@ -406,13 +416,12 @@
         )
         for k, (dy, dc) in enumerate(STEPS)
     ]
-    current = merge(orbit, parts)
-    filtered = from_rows(current, width)
-    gathered = lax.all_to_all(current.reshape(bands, planes, -1, 128), "band", 0, 0)
-    mixing = mixing_weights(coefficients, owners, width, bands)
-    turned = rotate(owners // width, mixing, gathered.reshape(bands, -1, 128))
-    returned = lax.all_to_all(turned.reshape(bands, planes, -1, 128), "band", 0, 0)
-    rotated = from_rows(returned.reshape(planes, tiles * width, 128), width)
+    homes = list(turned)
+    for k in (1, 3, 5, 7, 2, 4, 6):
+        homes[k] = lax.ppermute(turned[k], "band", [(i, i ^ k) for i in range(bands)])
+    filtered = from_rows(merge(orbit, parts), width)
+    rotated = place(jnp.arange(bands, dtype=jnp.int32) ^ place_b.astype(jnp.int32), homes)
+    rotated = from_rows(rotated.reshape(planes, tiles * width, 128), width)
     return (filtered, rotated)
 
 

time: 328 us -> 305 us (0.930)
  blocking collectives: 45.1 us -> 0 us
  starting transfers between devices: 32.6 us -> 44.9 us
  Pallas kernels: 75.9 us -> 84.8 us
  waiting for transfers between devices: 124 us -> 131 us
  local copies, waits for them, and re-layouts: 28.3 us -> 22.5 us
    all_to_all x1 -> x0, blocking collectives: 45.1 us -> none  [body(): lax.all_to_all(turned.reshape(bands, planes, -1, 128), 'band', 0, 0)]
    ppermute x0 -> x7, waiting for transfers between devices: none -> 39 us  [body(): lax.ppermute(turned[k], 'band', [(i, i ^ k) for i in range(bands)])]
    all_to_all x1, waiting for transfers between devices: 35.1 us -> 18.3 us  [body(): lax.all_to_all(current.reshape(4 * bands, -1, 128), AXES, 0, 0, axis_inde...]
    ppermute x19, waiting for transfers between devices: 88.5 us -> 73.3 us  [send(): return lax.ppermute(value, AXES, route(move))]
    ppermute x0 -> x7, starting transfers between devices: none -> 9.42 us  [body(): lax.ppermute(turned[k], 'band', [(i, i ^ k) for i in range(bands)])]
    pallas_call x2 -> x3, Pallas kernels: 12.5 us -> 21.4 us  [the longest x1 12.5 us: rotate(): pl.pallas_call(rotate_kernel, out_shape=[jax.ShapeDtypeStruct((tiles * 4,...]
  transfers between devices with their start and end apart: 20 -> 27, of which waited for: 10 -> 13; matrix products, arithmetic and copies ran while one was open for 6% -> 8% of each run, Pallas kernels for 17% -> 24%
where the time goes in v3:
time: 305 us; the launch traced here: 302 us
  waiting for transfers between devices  131 us (43%)
  Pallas kernels  84.8 us (28%)
  starting transfers between devices  44.9 us (15%)
  local copies, waits for them, and re-layouts  22.5 us (7%)
  other arithmetic  9.89 us (3%)
  between operations  9.16 us (3%)
    ppermute x19, waiting for transfers between devices, send(): return lax.ppermute(value, AXES, route(move))  73.3 us
    pallas_call x3, Pallas kernels, inner(): pl.pallas_call(functools.partial(inner_kernel, group=group, first=first),...  44 us
    ppermute x7, waiting for transfers between devices, body(): lax.ppermute(turned[k], 'band', [(i, i ^ k) for i in range(bands)])  39 us
    ppermute x19, starting transfers between devices, send(): return lax.ppermute(value, AXES, route(move))  28 us
    all_to_all x1, waiting for transfers between devices, body(): lax.all_to_all(current.reshape(4 * bands, -1, 128), AXES, 0, 0, axis_inde...  18.3 us
    pallas_call x1, Pallas kernels, rotate(): pl.pallas_call(rotate_kernel, out_shape=[jax.ShapeDtypeStruct((tiles * 4,...  12.5 us
    ppermute x7, starting transfers between devices, body(): lax.ppermute(turned[k], 'band', [(i, i ^ k) for i in range(bands)])  9.42 us
    pallas_call x2, Pallas kernels, place(): pl.pallas_call(place_kernel, out_shape=jax.ShapeDtypeStruct((first[0] * c...  8.93 us
  transfers between devices with their start and end apart: 27, of which 13 were waited for; matrix products, arithmetic and copies ran while one was open for 8% of the time, Pallas kernels for 24%

profile of v3, /device:TPU:16, one launch (start us, length us, event | category | flops | bytes accessed | tf_op | source)
XLA Modules:
  0.0 301.8 jit_solution(13672230273080161348)
XLA Ops:
  3.2 6.7 %collective-permute-done.4 = f32[432,128]{1,0:T(8,128)S(1)} collective-permute-done((f32[432,128]{1,0:T(8,128)S(1)}, f32[432,128]{1,0:T(8,128)S(1)}, u32[]{:S(2)}, u32[]{:S(2)}) %collective-permute-start.4) | collective-permute-done | bytes 221216 | tf_op jit(solution)/shard_map/ppermute | solution.py:327
  18.4 4.7 %collective-permute-done.6 = f32[432,128]{1,0:T(8,128)S(1)} collective-permute-done((f32[432,128]{1,0:T(8,128)S(1)}, f32[432,128]{1,0:T(8,128)S(1)}, u32[]{:S(2)}, u32[]{:S(2)}) %collective-permute-start.6) | collective-permute-done | bytes 221216 | tf_op jit(solution)/shard_map/ppermute | solution.py:327
  26.0 5.7 %split.1 = (f32[6,288,128]{2,1,0:T(8,128)}, f32[6,288,128]{2,1,0:T(8,128)}, f32[6,288,128]{2,1,0:T(8,128)}, f32[6,288,128]{2,1,0:T(8,128)}) custom-call(s32[4]{0:T(128)} %fusion.12.orbit, f32[6,1152,128]{2,1,0:T(8,128)} %bitcast.77), custom_call_target="tpu_custom_call" | custom-call | tf_op jit(solution)/shard_map/split/pallas_call | solution.py:251
  38.4 16.1 %collective-permute-done.refs_0_ = f32[6,288,128]{2,1,0:T(8,128)} collective-permute-done((f32[6,288,128]{2,1,0:T(8,128)}, f32[6,288,128]{2,1,0:T(8,128)}, u32[]{:S(2)}, u32[]{:S(2)}) %collective-permute-start) | collective-permute-done | bytes 884768 | tf_op jit(solution)/shard_map/ppermute | solution.py:327
  54.5 18.5 %collective-permute-done.1.refs_1_ = f32[6,288,128]{2,1,0:T(8,128)} collective-permute-done((f32[6,288,128]{2,1,0:T(8,128)}, f32[6,288,128]{2,1,0:T(8,128)}, u32[]{:S(2)}, u32[]{:S(2)}) %collective-permute-start.1) | collective-permute-done | bytes 884768 | tf_op jit(solution)/shard_map/ppermute | solution.py:327
  74.8 4.5 %place.2.own.rest_0_ = f32[24,288,128]{2,1,0:T(8,128)} custom-call(s32[4]{0:T(128)} %fusion.20.slot, f32[6,288,128]{2,1,0:T(8,128)} %collective-permute-done.refs_0_, f32[6,288,128]{2,1,0:T(8,128)} %collective-permute-done.1.refs_1_, f32[6,288,128]{2,1,0:T(8,128)} %collective-permute-done.2.refs_2_, f32[6,288,128]{2,1,0:T(8,128)} %collective-permute-done.3.refs_3_), custom_call_target="tpu_custom_call" | custom-call | tf_op jit(solution)/shard_map/place/pallas_call | solution.py:302
  81.7 5.9 %collective-permute-start.10 = (f32[4,288,128]{2,1,0:T(8,128)}, f32[4,288,128]{2,1,0:T(8,128)}, u32[]{:S(2)}, u32[]{:S(2)}) collective-permute-start(f32[4,288,128]{2,1,0:T(8,128)} %get-tuple-element.35), channel_id=1, source_target_pairs={{0,224},{2,226},{4,228},{6,230},{8,232},{10,234},{12,236},{14,238}... | collective-permute-start | bytes 1769480 | tf_op jit(solution)/shard_map/ppermute | solution.py:327
  90.9 13.7 %inner_first.1.partial = f32[24,288,128]{2,1,0:T(8,128)} custom-call(f32[24,288,128]{2,1,0:T(8,128)} %place.2.own.rest_0_, f32[24,288,128]{2,1,0:T(8,128)} %bitcast.68, bf16[1152,384]{1,0:T(8,128)(2,1)} %pad_maximum_fusion.2.line), custom_call_target="tpu_custom_call" | custom-call | tf_op jit(solution)/shard_map/inner_first/pallas_call | solution.py:134
  108.9 3.3 %collective-permute-start.12 = (f32[4,288,128]{2,1,0:T(8,128)S(1)}, f32[4,288,128]{2,1,0:T(8,128)S(1)}, u32[]{:S(2)}, u32[]{:S(2)}) collective-permute-start(f32[4,288,128]{2,1,0:T(8,128)S(1)} %get-tuple-element.33), channel_id=1, source_target_pairs={{0,224},{2,226},{4,228},{6,230},{8,232},{10,234},{12,236},{14,238}... | collective-permute-start | bytes 1769480 | tf_op jit(solution)/shard_map/ppermute | solution.py:327
  112.2 15.2 %inner_next.2.partial = f32[24,288,128]{2,1,0:T(8,128)} custom-call(f32[24,288,128]{2,1,0:T(8,128)} %edges.3.own.rest_0_, f32[24,288,128]{2,1,0:T(8,128)} %bitcast.69, bf16[1152,384]{1,0:T(8,128)(2,1)} %pad_maximum_fusion.2.line, f32[24,288,128]{2,1,0:T(8,128)} %place.2.own.rest_0_), custom_call_target="tpu_custom_call" | custom-call | tf_op jit(solution)/shard_map/inner_next/pallas_call | solution.py:134
  133.1 3.2 %collective-permute-start.14 = (f32[4,288,128]{2,1,0:T(8,128)S(1)}, f32[4,288,128]{2,1,0:T(8,128)S(1)}, u32[]{:S(2)}, u32[]{:S(2)}) collective-permute-start(f32[4,288,128]{2,1,0:T(8,128)S(1)} %get-tuple-element.31), channel_id=1, source_target_pairs={{0,224},{2,226},{4,228},{6,230},{8,232},{10,234},{12,236},{14,238}... | collective-permute-start | bytes 1769480 | tf_op jit(solution)/shard_map/ppermute | solution.py:327
  136.3 15.2 %inner_next.3.partial = f32[24,288,128]{2,1,0:T(8,128)} custom-call(f32[24,288,128]{2,1,0:T(8,128)} %edges.4.own, f32[24,288,128]{2,1,0:T(8,128)} %bitcast.70, bf16[1152,384]{1,0:T(8,128)(2,1)} %pad_maximum_fusion.2.line, f32[24,288,128]{2,1,0:T(8,128)} %edges.3.own.rest_0_), custom_call_target="tpu_custom_call" | custom-call | tf_op jit(solution)/shard_map/inner_next/pallas_call | solution.py:134
  155.8 7.4 %all-to-all-start = ((f32[32,216,128]{2,1,0:T(8,128)}), f32[32,216,128]{2,1,0:T(8,128)}, u32[]{:S(2)}, u32[]{:S(2)}) async-start(f32[32,216,128]{2,1,0:T(8,128)} %bitcast.71), calls=%async_computation | async-start | bytes 7077888 | tf_op jit(solution)/shard_map/all_to_all | solution.py:406
  188.7 18.3 %all-to-all-done.field = f32[32,216,128]{2,1,0:T(8,128)} async-done(((f32[32,216,128]{2,1,0:T(8,128)}), f32[32,216,128]{2,1,0:T(8,128)}, u32[]{:S(2)}, u32[]{:S(2)}) %all-to-all-start) | async-done | bytes 3538976 | tf_op jit(solution)/shard_map/all_to_all | solution.py:406
  207.0 12.5 %rotate.1 = (f32[864,128]{1,0:T(8,128)}, f32[864,128]{1,0:T(8,128)}, f32[864,128]{1,0:T(8,128)}, f32[864,128]{1,0:T(8,128)}, f32[864,128]{1,0:T(8,128)}, /*index...) custom-call(s32[3]{0:T(128)} %pad_add_fusion.picked, f32[3,8,4,4]{3,2,1,0:T(4,128)} %pad_maximum_fusion.3.mixing, ...), custom_call_target="tpu_custom_call" | custom-call | tf_op jit(solution)/shard_map/rotate/pallas_call | solution.py:220
  219.5 3.5 %collective-permute-start.19 = (f32[864,128]{1,0:T(8,128)}, f32[864,128]{1,0:T(8,128)}, u32[]{:S(2)}, u32[]{:S(2)}) collective-permute-start(f32[864,128]{1,0:T(8,128)} %get-tuple-element.20), channel_id=1, source_target_pairs={{0,1},{1,0},{2,3},{3,2},{4,5},{5,4},{6,7},{7,6},{8,9},{9,8},{10,11... | collective-permute-start | bytes 1327112 | tf_op jit(solution)/shard_map/ppermute | solution.py:421
  223.0 4.8 %collective-permute-done.15.refs_0_ = f32[6,288,128]{2,1,0:T(8,128)S(1)} collective-permute-done((f32[6,288,128]{2,1,0:T(8,128)}, f32[6,288,128]{2,1,0:T(8,128)S(1)}, u32[]{:S(2)}, u32[]{:S(2)}) %collective-permute-start.15) | collective-permute-done | bytes 884768 | tf_op jit(solution)/shard_map/ppermute | solution.py:327
  227.8 18.0 %collective-permute-done.16.refs_1_ = f32[6,288,128]{2,1,0:T(8,128)S(1)} collective-permute-done((f32[6,288,128]{2,1,0:T(8,128)}, f32[6,288,128]{2,1,0:T(8,128)S(1)}, u32[]{:S(2)}, u32[]{:S(2)}) %collective-permute-start.16) | collective-permute-done | bytes 884768 | tf_op jit(solution)/shard_map/ppermute | solution.py:327
  249.5 15.8 %collective-permute-done.19.refs_1_ = f32[864,128]{1,0:T(8,128)} collective-permute-done((f32[864,128]{1,0:T(8,128)}, f32[864,128]{1,0:T(8,128)}, u32[]{:S(2)}, u32[]{:S(2)}) %collective-permute-start.19) | collective-permute-done | bytes 442400 | tf_op jit(solution)/shard_map/ppermute | solution.py:421
  268.2 5.8 %merge.1 = f32[6,1152,128]{2,1,0:T(8,128)} custom-call(s32[4]{0:T(128)} %fusion.12.orbit, f32[6,288,128]{2,1,0:T(8,128)} %copy-done.3, f32[6,288,128]{2,1,0:T(8,128)} %copy-done.4, f32[6,288,128]{2,1,0:T(8,128)} %copy-done.5, f32[6,288,128]{2,1,0:T(8,128)} %copy-done.6), custom_call_target="tpu_custom_call" | custom-call | tf_op jit(solution)/shard_map/merge/pallas_call | solution.py:277
  274.0 4.3 %collective-permute-done.23.refs_5_ = f32[864,128]{1,0:T(8,128)} collective-permute-done((f32[864,128]{1,0:T(8,128)}, f32[864,128]{1,0:T(8,128)}, u32[]{:S(2)}, u32[]{:S(2)}) %collective-permute-start.23) | collective-permute-done | bytes 442400 | tf_op jit(solution)/shard_map/ppermute | solution.py:421
  278.3 8.4 %collective-permute-done.24.refs_6_ = f32[864,128]{1,0:T(8,128)} collective-permute-done((f32[864,128]{1,0:T(8,128)}, f32[864,128]{1,0:T(8,128)}, u32[]{:S(2)}, u32[]{:S(2)}) %collective-permute-start.24) | collective-permute-done | bytes 442400 | tf_op jit(solution)/shard_map/ppermute | solution.py:421
  286.8 10.4 %collective-permute-done.25.refs_7_ = f32[864,128]{1,0:T(8,128)} collective-permute-done((f32[864,128]{1,0:T(8,128)}, f32[864,128]{1,0:T(8,128)}, u32[]{:S(2)}, u32[]{:S(2)}) %collective-permute-start.25) | collective-permute-done | bytes 442400 | tf_op jit(solution)/shard_map/ppermute | solution.py:421
  297.2 4.5 %place.3 = f32[6912,128]{1,0:T(8,128)} custom-call(s32[8]{0:T(128)} %iota_xor_fusion.slot, f32[864,128]{1,0:T(8,128)} %get-tuple-element.19.refs_0_, f32[864,128]{1,0:T(8,128)} %collective-permute-done.19.refs_1_, f32[864,128]{1,0:T(8,128)} %collective-permute-done.20.refs_2_, f32[864,128]{1,0:T(8,128)} %collective-permute-done.21.refs_3_, ...), custom_call_target="tpu_custom_call" | custom-call | tf_op jit(solution)/shard_map/place/pallas_call | solution.py:302
  (115 shorter events, 66.2 us)
Async XLA Ops:
  11.4 11.8 %collective-permute-start.6 = (f32[432,128]{1,0:T(8,128)S(1)}, f32[432,128]{1,0:T(8,128)S(1)}, u32[]{:S(2)}, u32[]{:S(2)}) collective-permute-start(f32[432,128]{1,0:T(8,128)S(1)} %collective-permute-done.4), channel_id=1, source_target_pairs={{0,4},{2,6},{4,0},{6,2},{8,12},{10,14},{12,8},{14,10},{1,5},{3,7},... | collective-permute-start | bytes 663560 | tf_op jit(solution)/shard_map/ppermute | solution.py:327
  24.8 64.1 %collective-permute-start.8 = (f32[2,6,288,128]{3,2,1,0:T(8,128)}, f32[2,6,288,128]{3,2,1,0:T(8,128)S(1)}, u32[]{:S(2)}, u32[]{:S(2)}) collective-permute-start(f32[2,6,288,128]{3,2,1,0:T(8,128)} %maximum_select_fusion.2), channel_id=1, source_target_pairs={{0,8},{2,10},{4,12},{6,14},{8,0},{10,2},{12,4},{14,6},{1,9},{3,11}... | collective-permute-start | bytes 5308424 | tf_op jit(solution)/shard_map/ppermute | solution.py:327
  31.7 22.8 %collective-permute-start = (f32[6,288,128]{2,1,0:T(8,128)}, f32[6,288,128]{2,1,0:T(8,128)}, u32[]{:S(2)}, u32[]{:S(2)}) collective-permute-start(f32[6,288,128]{2,1,0:T(8,128)} %get-tuple-element.15), channel_id=1, source_target_pairs={{0,1},{2,3},{4,5},{6,7},{8,9},{10,11},{12,13},{14,15},{1,16},{3,18... | collective-permute-start | bytes 2654216 | tf_op jit(solution)/shard_map/ppermute | solution.py:327
  34.2 38.9 %collective-permute-start.1 = (f32[6,288,128]{2,1,0:T(8,128)}, f32[6,288,128]{2,1,0:T(8,128)}, u32[]{:S(2)}, u32[]{:S(2)}) collective-permute-start(f32[6,288,128]{2,1,0:T(8,128)} %get-tuple-element.16), channel_id=1, source_target_pairs={{0,9},{2,11},{4,13},{6,15},{8,1},{10,3},{12,5},{14,7},{1,24},{3,26... | collective-permute-start | bytes 2654216 | tf_op jit(solution)/shard_map/ppermute | solution.py:327
  34.3 38.7 %collective-permute-start.2 = (f32[6,288,128]{2,1,0:T(8,128)}, f32[6,288,128]{2,1,0:T(8,128)}, u32[]{:S(2)}, u32[]{:S(2)}) collective-permute-start(f32[6,288,128]{2,1,0:T(8,128)} %get-tuple-element.17), channel_id=1, source_target_pairs={{0,17},{2,19},{4,21},{6,23},{8,25},{10,27},{12,29},{14,31},{1,0},{... | collective-permute-start | bytes 2654216 | tf_op jit(solution)/shard_map/ppermute | solution.py:327
  36.0 38.7 %collective-permute-start.3 = (f32[6,288,128]{2,1,0:T(8,128)}, f32[6,288,128]{2,1,0:T(8,128)}, u32[]{:S(2)}, u32[]{:S(2)}) collective-permute-start(f32[6,288,128]{2,1,0:T(8,128)} %get-tuple-element.18), channel_id=1, source_target_pairs={{0,25},{2,27},{4,29},{6,31},{8,17},{10,19},{12,21},{14,23},{1,8},{... | collective-permute-start | bytes 2654216 | tf_op jit(solution)/shard_map/ppermute | solution.py:327
  81.7 22.9 %collective-permute-start.10 = (f32[4,288,128]{2,1,0:T(8,128)}, f32[4,288,128]{2,1,0:T(8,128)}, u32[]{:S(2)}, u32[]{:S(2)}) collective-permute-start(f32[4,288,128]{2,1,0:T(8,128)} %get-tuple-element.35), channel_id=1, source_target_pairs={{0,224},{2,226},{4,228},{6,230},{8,232},{10,234},{12,236},{14,238}... | collective-permute-start | bytes 1769480 | tf_op jit(solution)/shard_map/ppermute | solution.py:327
  87.5 17.1 %collective-permute-start.9 = (f32[4,288,128]{2,1,0:T(8,128)}, f32[4,288,128]{2,1,0:T(8,128)}, u32[]{:S(2)}, u32[]{:S(2)}) collective-permute-start(f32[4,288,128]{2,1,0:T(8,128)} %get-tuple-element.36), channel_id=1, source_target_pairs={{0,32},{2,34},{4,36},{6,38},{8,40},{10,42},{12,44},{14,46},{1,33},... | collective-permute-start | bytes 1769480 | tf_op jit(solution)/shard_map/ppermute | solution.py:327
  108.6 18.7 %collective-permute-start.11 = (f32[4,288,128]{2,1,0:T(8,128)S(1)}, f32[4,288,128]{2,1,0:T(8,128)S(1)}, u32[]{:S(2)}, u32[]{:S(2)}) collective-permute-start(f32[4,288,128]{2,1,0:T(8,128)S(1)} %get-tuple-element.34), channel_id=1, source_target_pairs={{0,32},{2,34},{4,36},{6,38},{8,40},{10,42},{12,44},{14,46},{1,33},... | collective-permute-start | bytes 1769480 | tf_op jit(solution)/shard_map/ppermute | solution.py:327
  108.9 18.5 %collective-permute-start.12 = (f32[4,288,128]{2,1,0:T(8,128)S(1)}, f32[4,288,128]{2,1,0:T(8,128)S(1)}, u32[]{:S(2)}, u32[]{:S(2)}) collective-permute-start(f32[4,288,128]{2,1,0:T(8,128)S(1)} %get-tuple-element.33), channel_id=1, source_target_pairs={{0,224},{2,226},{4,228},{6,230},{8,232},{10,234},{12,236},{14,238}... | collective-permute-start | bytes 1769480 | tf_op jit(solution)/shard_map/ppermute | solution.py:327
  133.0 18.5 %collective-permute-start.13 = (f32[4,288,128]{2,1,0:T(8,128)S(1)}, f32[4,288,128]{2,1,0:T(8,128)S(1)}, u32[]{:S(2)}, u32[]{:S(2)}) collective-permute-start(f32[4,288,128]{2,1,0:T(8,128)S(1)} %get-tuple-element.32), channel_id=1, source_target_pairs={{0,32},{2,34},{4,36},{6,38},{8,40},{10,42},{12,44},{14,46},{1,33},... | collective-permute-start | bytes 1769480 | tf_op jit(solution)/shard_map/ppermute | solution.py:327
  133.1 18.4 %collective-permute-start.14 = (f32[4,288,128]{2,1,0:T(8,128)S(1)}, f32[4,288,128]{2,1,0:T(8,128)S(1)}, u32[]{:S(2)}, u32[]{:S(2)}) collective-permute-start(f32[4,288,128]{2,1,0:T(8,128)S(1)} %get-tuple-element.31), channel_id=1, source_target_pairs={{0,224},{2,226},{4,228},{6,230},{8,232},{10,234},{12,236},{14,238}... | collective-permute-start | bytes 1769480 | tf_op jit(solution)/shard_map/ppermute | solution.py:327
  155.8 51.3 %all-to-all-start = ((f32[32,216,128]{2,1,0:T(8,128)}), f32[32,216,128]{2,1,0:T(8,128)}, u32[]{:S(2)}, u32[]{:S(2)}) async-start(f32[32,216,128]{2,1,0:T(8,128)} %bitcast.71), calls=%async_computation | async-start | bytes 7077888 | tf_op jit(solution)/shard_map/all_to_all | solution.py:406
  182.7 45.1 %collective-permute-start.15 = (f32[6,288,128]{2,1,0:T(8,128)}, f32[6,288,128]{2,1,0:T(8,128)S(1)}, u32[]{:S(2)}, u32[]{:S(2)}) collective-permute-start(f32[6,288,128]{2,1,0:T(8,128)} %get-tuple-element.30), channel_id=1, source_target_pairs={{0,17},{2,19},{4,21},{6,23},{8,25},{10,27},{12,29},{14,31},{1,0},{... | collective-permute-start | bytes 2654216 | tf_op jit(solution)/shard_map/ppermute | solution.py:327
  183.3 62.6 %collective-permute-start.16 = (f32[6,288,128]{2,1,0:T(8,128)}, f32[6,288,128]{2,1,0:T(8,128)S(1)}, u32[]{:S(2)}, u32[]{:S(2)}) collective-permute-start(f32[6,288,128]{2,1,0:T(8,128)} %get-tuple-element.29), channel_id=1, source_target_pairs={{0,25},{2,27},{4,29},{6,31},{8,17},{10,19},{12,21},{14,23},{1,8},{... | collective-permute-start | bytes 2654216 | tf_op jit(solution)/shard_map/ppermute | solution.py:327
  183.3 62.5 %collective-permute-start.17 = (f32[6,288,128]{2,1,0:T(8,128)}, f32[6,288,128]{2,1,0:T(8,128)S(1)}, u32[]{:S(2)}, u32[]{:S(2)}) collective-permute-start(f32[6,288,128]{2,1,0:T(8,128)} %get-tuple-element.28), channel_id=1, source_target_pairs={{0,1},{2,3},{4,5},{6,7},{8,9},{10,11},{12,13},{14,15},{1,16},{3,18... | collective-permute-start | bytes 2654216 | tf_op jit(solution)/shard_map/ppermute | solution.py:327
  184.9 62.1 %collective-permute-start.18 = (f32[6,288,128]{2,1,0:T(8,128)}, f32[6,288,128]{2,1,0:T(8,128)S(1)}, u32[]{:S(2)}, u32[]{:S(2)}) collective-permute-start(f32[6,288,128]{2,1,0:T(8,128)} %get-tuple-element.27), channel_id=1, source_target_pairs={{0,9},{2,11},{4,13},{6,15},{8,1},{10,3},{12,5},{14,7},{1,24},{3,26... | collective-permute-start | bytes 2654216 | tf_op jit(solution)/shard_map/ppermute | solution.py:327
  219.5 45.8 %collective-permute-start.19 = (f32[864,128]{1,0:T(8,128)}, f32[864,128]{1,0:T(8,128)}, u32[]{:S(2)}, u32[]{:S(2)}) collective-permute-start(f32[864,128]{1,0:T(8,128)} %get-tuple-element.20), channel_id=1, source_target_pairs={{0,1},{1,0},{2,3},{3,2},{4,5},{5,4},{6,7},{7,6},{8,9},{9,8},{10,11... | collective-permute-start | bytes 1327112 | tf_op jit(solution)/shard_map/ppermute | solution.py:421
  227.8 37.7 %collective-permute-start.20 = (f32[864,128]{1,0:T(8,128)}, f32[864,128]{1,0:T(8,128)}, u32[]{:S(2)}, u32[]{:S(2)}) collective-permute-start(f32[864,128]{1,0:T(8,128)} %get-tuple-element.21), channel_id=1, source_target_pairs={{0,2},{1,3},{2,0},{3,1},{4,6},{5,7},{6,4},{7,5},{8,10},{9,11},{10,... | collective-permute-start | bytes 1327112 | tf_op jit(solution)/shard_map/ppermute | solution.py:421
  245.8 28.2 %collective-permute-start.21 = (f32[864,128]{1,0:T(8,128)}, f32[864,128]{1,0:T(8,128)}, u32[]{:S(2)}, u32[]{:S(2)}) collective-permute-start(f32[864,128]{1,0:T(8,128)} %get-tuple-element.22), channel_id=1, source_target_pairs={{0,3},{1,2},{2,1},{3,0},{4,7},{5,6},{6,5},{7,4},{8,11},{9,10},{10,... | collective-permute-start | bytes 1327112 | tf_op jit(solution)/shard_map/ppermute | solution.py:421
  245.8 28.2 %collective-permute-start.22 = (f32[864,128]{1,0:T(8,128)}, f32[864,128]{1,0:T(8,128)}, u32[]{:S(2)}, u32[]{:S(2)}) collective-permute-start(f32[864,128]{1,0:T(8,128)} %get-tuple-element.23), channel_id=1, source_target_pairs={{0,4},{1,5},{2,6},{3,7},{4,0},{5,1},{6,2},{7,3},{8,12},{9,13},{10,... | collective-permute-start | bytes 1327112 | tf_op jit(solution)/shard_map/ppermute | solution.py:421
  247.0 31.3 %collective-permute-start.23 = (f32[864,128]{1,0:T(8,128)}, f32[864,128]{1,0:T(8,128)}, u32[]{:S(2)}, u32[]{:S(2)}) collective-permute-start(f32[864,128]{1,0:T(8,128)} %get-tuple-element.24), channel_id=1, source_target_pairs={{0,5},{1,4},{2,7},{3,6},{4,1},{5,0},{6,3},{7,2},{8,13},{9,12},{10,... | collective-permute-start | bytes 1327112 | tf_op jit(solution)/shard_map/ppermute | solution.py:421
  265.4 21.4 %collective-permute-start.24 = (f32[864,128]{1,0:T(8,128)}, f32[864,128]{1,0:T(8,128)}, u32[]{:S(2)}, u32[]{:S(2)}) collective-permute-start(f32[864,128]{1,0:T(8,128)} %get-tuple-element.25), channel_id=1, source_target_pairs={{0,6},{1,7},{2,4},{3,5},{4,2},{5,3},{6,0},{7,1},{8,14},{9,15},{10,... | collective-permute-start | bytes 1327112 | tf_op jit(solution)/shard_map/ppermute | solution.py:421
  265.5 31.7 %collective-permute-start.25 = (f32[864,128]{1,0:T(8,128)}, f32[864,128]{1,0:T(8,128)}, u32[]{:S(2)}, u32[]{:S(2)}) collective-permute-start(f32[864,128]{1,0:T(8,128)} %get-tuple-element.26), channel_id=1, source_target_pairs={{0,7},{1,6},{2,5},{3,4},{4,3},{5,2},{6,1},{7,0},{8,15},{9,14},{10,... | collective-permute-start | bytes 1327112 | tf_op jit(solution)/shard_map/ppermute | solution.py:421
  (18 other events, 211.4 us)

commit v4 on v3

--- a/solution.py
+++ b/solution.py
@@ -199,15 +199,14 @@
 
         shared = members(picked[0]) + members(picked[1])
         for k, out in enumerate(outs):
-            band = picked[2] ^ k
-            own = members(band)
+            own = members(picked[2] ^ k)
             for o in range(4):
-                total = mixing[0, band, 0, o] * own[0]
+                total = mixing[0, k, 0, o] * own[0]
                 for q in range(1, 4):
-                    total = total + mixing[0, band, q, o] * own[q]
+                    total = total + mixing[0, k, q, o] * own[q]
                 for t in range(2):
                     for q in range(4):
-                        total = total + mixing[1 + t, band, q, o] * shared[4 * t + q]
+                        total = total + mixing[1 + t, k, q, o] * shared[4 * t + q]
                 out[pl.ds(i * 32 + o, 8, stride=4), :] = total
         return carry
 
@@ -407,6 +406,9 @@
         current.reshape(4 * bands, -1, 128), AXES, 0, 0, axis_index_groups=layer, tiled=True
     )
     mixing = mixing_weights(coefficients, owners, width, bands)
+    mixing = jnp.concatenate(
+        [lax.dynamic_slice_in_dim(mixing, place_b.astype(jnp.int32) ^ k, 1, 1) for k in range(bands)], axis=1
+    )
     picked = jnp.concatenate([owners // width, place_b[None].astype(jnp.int32)])
     turned = rotate(picked, mixing, gathered)
     parts = [

time: 305 us -> 305 us (level)
  local copies, waits for them, and re-layouts: 22.5 us -> 27 us
    ppermute x19, waiting for transfers between devices: 73.3 us -> 79.1 us  [send(): return lax.ppermute(value, AXES, route(move))]
    unnamed x38 -> x41, local copies, waits for them, and re-layouts: 3.63 us -> 7.7 us
    all_to_all x1, waiting for transfers between devices: 18.3 us -> 14.3 us  [body(): lax.all_to_all(current.reshape(4 * bands, -1, 128), AXES, 0, 0, axis_inde...]
  transfers between devices with their start and end apart: 27 -> 27, of which waited for: 13 -> 14; matrix products, arithmetic and copies ran while one was open for 8% -> 9% of each run, Pallas kernels for 24% -> 23%
where the time goes in v4:
time: 305 us; the launch traced here: 303 us
  waiting for transfers between devices  132 us (43%)
  Pallas kernels  82 us (27%)
  starting transfers between devices  42.9 us (14%)
  local copies, waits for them, and re-layouts  27 us (9%)
  other arithmetic  9.89 us (3%)
  between operations  8.47 us (3%)
    ppermute x19, waiting for transfers between devices, send(): return lax.ppermute(value, AXES, route(move))  79.1 us
    pallas_call x3, Pallas kernels, inner(): pl.pallas_call(functools.partial(inner_kernel, group=group, first=first),...  44 us
    ppermute x7, waiting for transfers between devices, body(): lax.ppermute(turned[k], 'band', [(i, i ^ k) for i in range(bands)])  38.9 us
    ppermute x19, starting transfers between devices, send(): return lax.ppermute(value, AXES, route(move))  26.8 us
    all_to_all x1, waiting for transfers between devices, body(): lax.all_to_all(current.reshape(4 * bands, -1, 128), AXES, 0, 0, axis_inde...  14.3 us
    pallas_call x1, Pallas kernels, rotate(): pl.pallas_call(rotate_kernel, out_shape=[jax.ShapeDtypeStruct((tiles * 4,...  9.72 us
    ppermute x7, starting transfers between devices, body(): lax.ppermute(turned[k], 'band', [(i, i ^ k) for i in range(bands)])  9.71 us
    pallas_call x2, Pallas kernels, place(): pl.pallas_call(place_kernel, out_shape=jax.ShapeDtypeStruct((first[0] * c...  8.93 us
  transfers between devices with their start and end apart: 27, of which 14 were waited for; matrix products, arithmetic and copies ran while one was open for 9% of the time, Pallas kernels for 23%

profile of v4, /device:TPU:16, one launch (start us, length us, event | category | flops | bytes accessed | tf_op | source)
XLA Modules:
  0.0 302.5 jit_solution(16724570170603224945)
XLA Ops:
  3.2 6.7 %collective-permute-done.4 = f32[432,128]{1,0:T(8,128)S(1)} collective-permute-done((f32[432,128]{1,0:T(8,128)S(1)}, f32[432,128]{1,0:T(8,128)S(1)}, u32[]{:S(2)}, u32[]{:S(2)}) %collective-permute-start.4) | collective-permute-done | bytes 221216 | tf_op jit(solution)/shard_map/ppermute | solution.py:326
  14.6 6.7 %collective-permute-done.7 = f32[432,128]{1,0:T(8,128)S(1)} collective-permute-done((f32[432,128]{1,0:T(8,128)S(1)}, f32[432,128]{1,0:T(8,128)S(1)}, u32[]{:S(2)}, u32[]{:S(2)}) %collective-permute-start.7) | collective-permute-done | bytes 221216 | tf_op jit(solution)/shard_map/ppermute | solution.py:326
  27.8 5.7 %split.1 = (f32[6,288,128]{2,1,0:T(8,128)}, f32[6,288,128]{2,1,0:T(8,128)}, f32[6,288,128]{2,1,0:T(8,128)}, f32[6,288,128]{2,1,0:T(8,128)}) custom-call(s32[4]{0:T(128)} %fusion.12.orbit, f32[6,1152,128]{2,1,0:T(8,128)} %bitcast.77), custom_call_target="tpu_custom_call" | custom-call | tf_op jit(solution)/shard_map/split/pallas_call | solution.py:250
  40.1 16.2 %collective-permute-done.refs_0_ = f32[6,288,128]{2,1,0:T(8,128)} collective-permute-done((f32[6,288,128]{2,1,0:T(8,128)}, f32[6,288,128]{2,1,0:T(8,128)}, u32[]{:S(2)}, u32[]{:S(2)}) %collective-permute-start) | collective-permute-done | bytes 884768 | tf_op jit(solution)/shard_map/ppermute | solution.py:326
  56.3 18.5 %collective-permute-done.1.refs_1_ = f32[6,288,128]{2,1,0:T(8,128)} collective-permute-done((f32[6,288,128]{2,1,0:T(8,128)}, f32[6,288,128]{2,1,0:T(8,128)}, u32[]{:S(2)}, u32[]{:S(2)}) %collective-permute-start.1) | collective-permute-done | bytes 884768 | tf_op jit(solution)/shard_map/ppermute | solution.py:326
  76.6 4.5 %place.2.own.rest_0_ = f32[24,288,128]{2,1,0:T(8,128)} custom-call(s32[4]{0:T(128)} %fusion.20.slot, f32[6,288,128]{2,1,0:T(8,128)} %collective-permute-done.refs_0_, f32[6,288,128]{2,1,0:T(8,128)} %collective-permute-done.1.refs_1_, f32[6,288,128]{2,1,0:T(8,128)} %collective-permute-done.2.refs_2_, f32[6,288,128]{2,1,0:T(8,128)} %collective-permute-done.3.refs_3_), custom_call_target="tpu_custom_call" | custom-call | tf_op jit(solution)/shard_map/place/pallas_call | solution.py:301
  85.4 3.9 %collective-permute-start.10 = (f32[4,288,128]{2,1,0:T(8,128)}, f32[4,288,128]{2,1,0:T(8,128)}, u32[]{:S(2)}, u32[]{:S(2)}) collective-permute-start(f32[4,288,128]{2,1,0:T(8,128)} %get-tuple-element.35), channel_id=1, source_target_pairs={{0,224},{2,226},{4,228},{6,230},{8,232},{10,234},{12,236},{14,238}... | collective-permute-start | bytes 1769480 | tf_op jit(solution)/shard_map/ppermute | solution.py:326
  92.8 13.6 %inner_first.1.partial = f32[24,288,128]{2,1,0:T(8,128)} custom-call(f32[24,288,128]{2,1,0:T(8,128)} %place.2.own.rest_0_, f32[24,288,128]{2,1,0:T(8,128)} %bitcast.68, bf16[1152,384]{1,0:T(8,128)(2,1)} %pad_maximum_fusion.2.line), custom_call_target="tpu_custom_call" | custom-call | tf_op jit(solution)/shard_map/inner_first/pallas_call | solution.py:134
  110.6 3.2 %collective-permute-start.12 = (f32[4,288,128]{2,1,0:T(8,128)S(1)}, f32[4,288,128]{2,1,0:T(8,128)S(1)}, u32[]{:S(2)}, u32[]{:S(2)}) collective-permute-start(f32[4,288,128]{2,1,0:T(8,128)S(1)} %get-tuple-element.33), channel_id=1, source_target_pairs={{0,224},{2,226},{4,228},{6,230},{8,232},{10,234},{12,236},{14,238}... | collective-permute-start | bytes 1769480 | tf_op jit(solution)/shard_map/ppermute | solution.py:326
  113.9 15.2 %inner_next.2.partial = f32[24,288,128]{2,1,0:T(8,128)} custom-call(f32[24,288,128]{2,1,0:T(8,128)} %edges.3.own.rest_0_, f32[24,288,128]{2,1,0:T(8,128)} %bitcast.69, bf16[1152,384]{1,0:T(8,128)(2,1)} %pad_maximum_fusion.2.line, f32[24,288,128]{2,1,0:T(8,128)} %place.2.own.rest_0_), custom_call_target="tpu_custom_call" | custom-call | tf_op jit(solution)/shard_map/inner_next/pallas_call | solution.py:134
  134.8 3.2 %collective-permute-start.14 = (f32[4,288,128]{2,1,0:T(8,128)S(1)}, f32[4,288,128]{2,1,0:T(8,128)S(1)}, u32[]{:S(2)}, u32[]{:S(2)}) collective-permute-start(f32[4,288,128]{2,1,0:T(8,128)S(1)} %get-tuple-element.31), channel_id=1, source_target_pairs={{0,224},{2,226},{4,228},{6,230},{8,232},{10,234},{12,236},{14,238}... | collective-permute-start | bytes 1769480 | tf_op jit(solution)/shard_map/ppermute | solution.py:326
  138.0 15.2 %inner_next.3.partial = f32[24,288,128]{2,1,0:T(8,128)} custom-call(f32[24,288,128]{2,1,0:T(8,128)} %edges.4.own, f32[24,288,128]{2,1,0:T(8,128)} %bitcast.70, bf16[1152,384]{1,0:T(8,128)(2,1)} %pad_maximum_fusion.2.line, f32[24,288,128]{2,1,0:T(8,128)} %edges.3.own.rest_0_), custom_call_target="tpu_custom_call" | custom-call | tf_op jit(solution)/shard_map/inner_next/pallas_call | solution.py:134
  157.4 6.4 %all-to-all-start = ((f32[32,216,128]{2,1,0:T(8,128)}), f32[32,216,128]{2,1,0:T(8,128)}, u32[]{:S(2)}, u32[]{:S(2)}) async-start(f32[32,216,128]{2,1,0:T(8,128)} %bitcast.71), calls=%async_computation | async-start | bytes 7077888 | tf_op jit(solution)/shard_map/all_to_all | solution.py:405
  193.4 14.3 %all-to-all-done.field = f32[32,216,128]{2,1,0:T(8,128)} async-done(((f32[32,216,128]{2,1,0:T(8,128)}), f32[32,216,128]{2,1,0:T(8,128)}, u32[]{:S(2)}, u32[]{:S(2)}) %all-to-all-start) | async-done | bytes 3538976 | tf_op jit(solution)/shard_map/all_to_all | solution.py:405
  207.8 9.7 %rotate.1 = (f32[864,128]{1,0:T(8,128)}, f32[864,128]{1,0:T(8,128)}, f32[864,128]{1,0:T(8,128)}, f32[864,128]{1,0:T(8,128)}, f32[864,128]{1,0:T(8,128)}, /*index...) custom-call(s32[3]{0:T(128)} %pad_add_fusion.picked, ...), custom_call_target="tpu_custom_call" | custom-call | tf_op jit(solution)/shard_map/rotate/pallas_call | solution.py:219
  217.5 3.6 %collective-permute-start.19 = (f32[864,128]{1,0:T(8,128)}, f32[864,128]{1,0:T(8,128)}, u32[]{:S(2)}, u32[]{:S(2)}) collective-permute-start(f32[864,128]{1,0:T(8,128)} %get-tuple-element.20), channel_id=1, source_target_pairs={{0,1},{1,0},{2,3},{3,2},{4,5},{5,4},{6,7},{7,6},{8,9},{9,8},{10,11... | collective-permute-start | bytes 1327112 | tf_op jit(solution)/shard_map/ppermute | solution.py:423
  221.1 7.5 %collective-permute-done.15.refs_0_ = f32[6,288,128]{2,1,0:T(8,128)S(1)} collective-permute-done((f32[6,288,128]{2,1,0:T(8,128)}, f32[6,288,128]{2,1,0:T(8,128)S(1)}, u32[]{:S(2)}, u32[]{:S(2)}) %collective-permute-start.15) | collective-permute-done | bytes 884768 | tf_op jit(solution)/shard_map/ppermute | solution.py:326
  228.5 18.0 %collective-permute-done.16.refs_1_ = f32[6,288,128]{2,1,0:T(8,128)S(1)} collective-permute-done((f32[6,288,128]{2,1,0:T(8,128)}, f32[6,288,128]{2,1,0:T(8,128)S(1)}, u32[]{:S(2)}, u32[]{:S(2)}) %collective-permute-start.16) | collective-permute-done | bytes 884768 | tf_op jit(solution)/shard_map/ppermute | solution.py:326
  250.5 15.6 %collective-permute-done.19.refs_1_ = f32[864,128]{1,0:T(8,128)} collective-permute-done((f32[864,128]{1,0:T(8,128)}, f32[864,128]{1,0:T(8,128)}, u32[]{:S(2)}, u32[]{:S(2)}) %collective-permute-start.19) | collective-permute-done | bytes 442400 | tf_op jit(solution)/shard_map/ppermute | solution.py:423
  268.8 5.8 %merge.1 = f32[6,1152,128]{2,1,0:T(8,128)} custom-call(s32[4]{0:T(128)} %fusion.12.orbit, f32[6,288,128]{2,1,0:T(8,128)} %copy-done.3, f32[6,288,128]{2,1,0:T(8,128)} %copy-done.4, f32[6,288,128]{2,1,0:T(8,128)} %copy-done.5, f32[6,288,128]{2,1,0:T(8,128)} %copy-done.6), custom_call_target="tpu_custom_call" | custom-call | tf_op jit(solution)/shard_map/merge/pallas_call | solution.py:276
  274.7 4.4 %collective-permute-done.23.refs_5_ = f32[864,128]{1,0:T(8,128)} collective-permute-done((f32[864,128]{1,0:T(8,128)}, f32[864,128]{1,0:T(8,128)}, u32[]{:S(2)}, u32[]{:S(2)}) %collective-permute-start.23) | collective-permute-done | bytes 442400 | tf_op jit(solution)/shard_map/ppermute | solution.py:423
  279.0 8.9 %collective-permute-done.24.refs_6_ = f32[864,128]{1,0:T(8,128)} collective-permute-done((f32[864,128]{1,0:T(8,128)}, f32[864,128]{1,0:T(8,128)}, u32[]{:S(2)}, u32[]{:S(2)}) %collective-permute-start.24) | collective-permute-done | bytes 442400 | tf_op jit(solution)/shard_map/ppermute | solution.py:423
  287.9 10.0 %collective-permute-done.25.refs_7_ = f32[864,128]{1,0:T(8,128)} collective-permute-done((f32[864,128]{1,0:T(8,128)}, f32[864,128]{1,0:T(8,128)}, u32[]{:S(2)}, u32[]{:S(2)}) %collective-permute-start.25) | collective-permute-done | bytes 442400 | tf_op jit(solution)/shard_map/ppermute | solution.py:423
  297.9 4.5 %place.3 = f32[6912,128]{1,0:T(8,128)} custom-call(s32[8]{0:T(128)} %iota_xor_fusion.slot, f32[864,128]{1,0:T(8,128)} %get-tuple-element.19.refs_0_, f32[864,128]{1,0:T(8,128)} %collective-permute-done.19.refs_1_, f32[864,128]{1,0:T(8,128)} %collective-permute-done.20.refs_2_, f32[864,128]{1,0:T(8,128)} %collective-permute-done.21.refs_3_, ...), custom_call_target="tpu_custom_call" | custom-call | tf_op jit(solution)/shard_map/place/pallas_call | solution.py:301
  (119 shorter events, 72.7 us)
Async XLA Ops:
  13.5 11.5 %collective-permute-start.5 = (f32[432,128]{1,0:T(8,128)S(1)}, f32[432,128]{1,0:T(8,128)S(1)}, u32[]{:S(2)}, u32[]{:S(2)}) collective-permute-start(f32[432,128]{1,0:T(8,128)S(1)} %collective-permute-done.4), channel_id=1, source_target_pairs={{0,2},{2,4},{4,6},{6,0},{8,10},{10,12},{12,14},{14,8},{1,3},{3,5},... | collective-permute-start | bytes 663560 | tf_op jit(solution)/shard_map/ppermute | solution.py:326
  26.5 64.1 %collective-permute-start.8 = (f32[2,6,288,128]{3,2,1,0:T(8,128)}, f32[2,6,288,128]{3,2,1,0:T(8,128)S(1)}, u32[]{:S(2)}, u32[]{:S(2)}) collective-permute-start(f32[2,6,288,128]{3,2,1,0:T(8,128)} %maximum_select_fusion.2), channel_id=1, source_target_pairs={{0,8},{2,10},{4,12},{6,14},{8,0},{10,2},{12,4},{14,6},{1,9},{3,11}... | collective-permute-start | bytes 5308424 | tf_op jit(solution)/shard_map/ppermute | solution.py:326
  33.5 22.8 %collective-permute-start = (f32[6,288,128]{2,1,0:T(8,128)}, f32[6,288,128]{2,1,0:T(8,128)}, u32[]{:S(2)}, u32[]{:S(2)}) collective-permute-start(f32[6,288,128]{2,1,0:T(8,128)} %get-tuple-element.15), channel_id=1, source_target_pairs={{0,1},{2,3},{4,5},{6,7},{8,9},{10,11},{12,13},{14,15},{1,16},{3,18... | collective-permute-start | bytes 2654216 | tf_op jit(solution)/shard_map/ppermute | solution.py:326
  36.0 38.9 %collective-permute-start.1 = (f32[6,288,128]{2,1,0:T(8,128)}, f32[6,288,128]{2,1,0:T(8,128)}, u32[]{:S(2)}, u32[]{:S(2)}) collective-permute-start(f32[6,288,128]{2,1,0:T(8,128)} %get-tuple-element.16), channel_id=1, source_target_pairs={{0,9},{2,11},{4,13},{6,15},{8,1},{10,3},{12,5},{14,7},{1,24},{3,26... | collective-permute-start | bytes 2654216 | tf_op jit(solution)/shard_map/ppermute | solution.py:326
  36.1 38.7 %collective-permute-start.2 = (f32[6,288,128]{2,1,0:T(8,128)}, f32[6,288,128]{2,1,0:T(8,128)}, u32[]{:S(2)}, u32[]{:S(2)}) collective-permute-start(f32[6,288,128]{2,1,0:T(8,128)} %get-tuple-element.17), channel_id=1, source_target_pairs={{0,17},{2,19},{4,21},{6,23},{8,25},{10,27},{12,29},{14,31},{1,0},{... | collective-permute-start | bytes 2654216 | tf_op jit(solution)/shard_map/ppermute | solution.py:326
  37.8 38.8 %collective-permute-start.3 = (f32[6,288,128]{2,1,0:T(8,128)}, f32[6,288,128]{2,1,0:T(8,128)}, u32[]{:S(2)}, u32[]{:S(2)}) collective-permute-start(f32[6,288,128]{2,1,0:T(8,128)} %get-tuple-element.18), channel_id=1, source_target_pairs={{0,25},{2,27},{4,29},{6,31},{8,17},{10,19},{12,21},{14,23},{1,8},{... | collective-permute-start | bytes 2654216 | tf_op jit(solution)/shard_map/ppermute | solution.py:326
  83.5 22.9 %collective-permute-start.9 = (f32[4,288,128]{2,1,0:T(8,128)}, f32[4,288,128]{2,1,0:T(8,128)}, u32[]{:S(2)}, u32[]{:S(2)}) collective-permute-start(f32[4,288,128]{2,1,0:T(8,128)} %get-tuple-element.36), channel_id=1, source_target_pairs={{0,32},{2,34},{4,36},{6,38},{8,40},{10,42},{12,44},{14,46},{1,33},... | collective-permute-start | bytes 1769480 | tf_op jit(solution)/shard_map/ppermute | solution.py:326
  85.4 21.0 %collective-permute-start.10 = (f32[4,288,128]{2,1,0:T(8,128)}, f32[4,288,128]{2,1,0:T(8,128)}, u32[]{:S(2)}, u32[]{:S(2)}) collective-permute-start(f32[4,288,128]{2,1,0:T(8,128)} %get-tuple-element.35), channel_id=1, source_target_pairs={{0,224},{2,226},{4,228},{6,230},{8,232},{10,234},{12,236},{14,238}... | collective-permute-start | bytes 1769480 | tf_op jit(solution)/shard_map/ppermute | solution.py:326
  110.4 18.7 %collective-permute-start.11 = (f32[4,288,128]{2,1,0:T(8,128)S(1)}, f32[4,288,128]{2,1,0:T(8,128)S(1)}, u32[]{:S(2)}, u32[]{:S(2)}) collective-permute-start(f32[4,288,128]{2,1,0:T(8,128)S(1)} %get-tuple-element.34), channel_id=1, source_target_pairs={{0,32},{2,34},{4,36},{6,38},{8,40},{10,42},{12,44},{14,46},{1,33},... | collective-permute-start | bytes 1769480 | tf_op jit(solution)/shard_map/ppermute | solution.py:326
  110.6 18.4 %collective-permute-start.12 = (f32[4,288,128]{2,1,0:T(8,128)S(1)}, f32[4,288,128]{2,1,0:T(8,128)S(1)}, u32[]{:S(2)}, u32[]{:S(2)}) collective-permute-start(f32[4,288,128]{2,1,0:T(8,128)S(1)} %get-tuple-element.33), channel_id=1, source_target_pairs={{0,224},{2,226},{4,228},{6,230},{8,232},{10,234},{12,236},{14,238}... | collective-permute-start | bytes 1769480 | tf_op jit(solution)/shard_map/ppermute | solution.py:326
  134.7 18.5 %collective-permute-start.13 = (f32[4,288,128]{2,1,0:T(8,128)S(1)}, f32[4,288,128]{2,1,0:T(8,128)S(1)}, u32[]{:S(2)}, u32[]{:S(2)}) collective-permute-start(f32[4,288,128]{2,1,0:T(8,128)S(1)} %get-tuple-element.32), channel_id=1, source_target_pairs={{0,32},{2,34},{4,36},{6,38},{8,40},{10,42},{12,44},{14,46},{1,33},... | collective-permute-start | bytes 1769480 | tf_op jit(solution)/shard_map/ppermute | solution.py:326
  134.8 18.4 %collective-permute-start.14 = (f32[4,288,128]{2,1,0:T(8,128)S(1)}, f32[4,288,128]{2,1,0:T(8,128)S(1)}, u32[]{:S(2)}, u32[]{:S(2)}) collective-permute-start(f32[4,288,128]{2,1,0:T(8,128)S(1)} %get-tuple-element.31), channel_id=1, source_target_pairs={{0,224},{2,226},{4,228},{6,230},{8,232},{10,234},{12,236},{14,238}... | collective-permute-start | bytes 1769480 | tf_op jit(solution)/shard_map/ppermute | solution.py:326
  157.4 50.3 %all-to-all-start = ((f32[32,216,128]{2,1,0:T(8,128)}), f32[32,216,128]{2,1,0:T(8,128)}, u32[]{:S(2)}, u32[]{:S(2)}) async-start(f32[32,216,128]{2,1,0:T(8,128)} %bitcast.71), calls=%async_computation | async-start | bytes 7077888 | tf_op jit(solution)/shard_map/all_to_all | solution.py:405
  185.1 43.5 %collective-permute-start.15 = (f32[6,288,128]{2,1,0:T(8,128)}, f32[6,288,128]{2,1,0:T(8,128)S(1)}, u32[]{:S(2)}, u32[]{:S(2)}) collective-permute-start(f32[6,288,128]{2,1,0:T(8,128)} %get-tuple-element.30), channel_id=1, source_target_pairs={{0,17},{2,19},{4,21},{6,23},{8,25},{10,27},{12,29},{14,31},{1,0},{... | collective-permute-start | bytes 2654216 | tf_op jit(solution)/shard_map/ppermute | solution.py:326
  186.8 59.8 %collective-permute-start.16 = (f32[6,288,128]{2,1,0:T(8,128)}, f32[6,288,128]{2,1,0:T(8,128)S(1)}, u32[]{:S(2)}, u32[]{:S(2)}) collective-permute-start(f32[6,288,128]{2,1,0:T(8,128)} %get-tuple-element.29), channel_id=1, source_target_pairs={{0,25},{2,27},{4,29},{6,31},{8,17},{10,19},{12,21},{14,23},{1,8},{... | collective-permute-start | bytes 2654216 | tf_op jit(solution)/shard_map/ppermute | solution.py:326
  186.8 60.2 %collective-permute-start.17 = (f32[6,288,128]{2,1,0:T(8,128)}, f32[6,288,128]{2,1,0:T(8,128)S(1)}, u32[]{:S(2)}, u32[]{:S(2)}) collective-permute-start(f32[6,288,128]{2,1,0:T(8,128)} %get-tuple-element.28), channel_id=1, source_target_pairs={{0,1},{2,3},{4,5},{6,7},{8,9},{10,11},{12,13},{14,15},{1,16},{3,18... | collective-permute-start | bytes 2654216 | tf_op jit(solution)/shard_map/ppermute | solution.py:326
  188.5 60.4 %collective-permute-start.18 = (f32[6,288,128]{2,1,0:T(8,128)}, f32[6,288,128]{2,1,0:T(8,128)S(1)}, u32[]{:S(2)}, u32[]{:S(2)}) collective-permute-start(f32[6,288,128]{2,1,0:T(8,128)} %get-tuple-element.27), channel_id=1, source_target_pairs={{0,9},{2,11},{4,13},{6,15},{8,1},{10,3},{12,5},{14,7},{1,24},{3,26... | collective-permute-start | bytes 2654216 | tf_op jit(solution)/shard_map/ppermute | solution.py:326
  217.5 48.6 %collective-permute-start.19 = (f32[864,128]{1,0:T(8,128)}, f32[864,128]{1,0:T(8,128)}, u32[]{:S(2)}, u32[]{:S(2)}) collective-permute-start(f32[864,128]{1,0:T(8,128)} %get-tuple-element.20), channel_id=1, source_target_pairs={{0,1},{1,0},{2,3},{3,2},{4,5},{5,4},{6,7},{7,6},{8,9},{9,8},{10,11... | collective-permute-start | bytes 1327112 | tf_op jit(solution)/shard_map/ppermute | solution.py:423
  228.5 37.7 %collective-permute-start.20 = (f32[864,128]{1,0:T(8,128)}, f32[864,128]{1,0:T(8,128)}, u32[]{:S(2)}, u32[]{:S(2)}) collective-permute-start(f32[864,128]{1,0:T(8,128)} %get-tuple-element.21), channel_id=1, source_target_pairs={{0,2},{1,3},{2,0},{3,1},{4,6},{5,7},{6,4},{7,5},{8,10},{9,11},{10,... | collective-permute-start | bytes 1327112 | tf_op jit(solution)/shard_map/ppermute | solution.py:423
  246.6 28.1 %collective-permute-start.21 = (f32[864,128]{1,0:T(8,128)}, f32[864,128]{1,0:T(8,128)}, u32[]{:S(2)}, u32[]{:S(2)}) collective-permute-start(f32[864,128]{1,0:T(8,128)} %get-tuple-element.22), channel_id=1, source_target_pairs={{0,3},{1,2},{2,1},{3,0},{4,7},{5,6},{6,5},{7,4},{8,11},{9,10},{10,... | collective-permute-start | bytes 1327112 | tf_op jit(solution)/shard_map/ppermute | solution.py:423
  247.0 27.6 %collective-permute-start.22 = (f32[864,128]{1,0:T(8,128)}, f32[864,128]{1,0:T(8,128)}, u32[]{:S(2)}, u32[]{:S(2)}) collective-permute-start(f32[864,128]{1,0:T(8,128)} %get-tuple-element.23), channel_id=1, source_target_pairs={{0,4},{1,5},{2,6},{3,7},{4,0},{5,1},{6,2},{7,3},{8,12},{9,13},{10,... | collective-permute-start | bytes 1327112 | tf_op jit(solution)/shard_map/ppermute | solution.py:423
  248.9 30.2 %collective-permute-start.23 = (f32[864,128]{1,0:T(8,128)}, f32[864,128]{1,0:T(8,128)}, u32[]{:S(2)}, u32[]{:S(2)}) collective-permute-start(f32[864,128]{1,0:T(8,128)} %get-tuple-element.24), channel_id=1, source_target_pairs={{0,5},{1,4},{2,7},{3,6},{4,1},{5,0},{6,3},{7,2},{8,13},{9,12},{10,... | collective-permute-start | bytes 1327112 | tf_op jit(solution)/shard_map/ppermute | solution.py:423
  266.1 21.8 %collective-permute-start.24 = (f32[864,128]{1,0:T(8,128)}, f32[864,128]{1,0:T(8,128)}, u32[]{:S(2)}, u32[]{:S(2)}) collective-permute-start(f32[864,128]{1,0:T(8,128)} %get-tuple-element.25), channel_id=1, source_target_pairs={{0,6},{1,7},{2,4},{3,5},{4,2},{5,3},{6,0},{7,1},{8,14},{9,15},{10,... | collective-permute-start | bytes 1327112 | tf_op jit(solution)/shard_map/ppermute | solution.py:423
  266.2 31.7 %collective-permute-start.25 = (f32[864,128]{1,0:T(8,128)}, f32[864,128]{1,0:T(8,128)}, u32[]{:S(2)}, u32[]{:S(2)}) collective-permute-start(f32[864,128]{1,0:T(8,128)} %get-tuple-element.26), channel_id=1, source_target_pairs={{0,7},{1,6},{2,5},{3,4},{4,3},{5,2},{6,1},{7,0},{8,15},{9,14},{10,... | collective-permute-start | bytes 1327112 | tf_op jit(solution)/shard_map/ppermute | solution.py:423
  (16 other events, 198.5 us)
